TPU v7x, 512 devices: a whole 4x4x16 slice. The times are simulated.
512 devices in a mesh: lon: 16 (over x, y), sec: 32 (over z, core).
Axes of the slice: x: 4, y: 4, z: 16, core: 2. Of those that a mesh axis runs over, the one named last changes fastest.
Arguments:
- moisture: float32 [16, 512, 4096], P(None, 'sec', 'lon'), may hold values from 0 to 2
- heat: float32 [16, 512, 4096], P(None, 'sec', 'lon'), may hold values from -6 to 6
- moist_cond: float32 [16, 512, 4096], P(None, 'sec', 'lon'), may hold values from 0.05 to 2
- heat_cond: float32 [16, 512, 4096], P(None, 'sec', 'lon'), may hold values from 0.1 to 3
- rain: float32 [512, 4096], P('sec', 'lon'), may hold values from 0.01 to 1
- surface_flux: float32 [512, 4096], P('sec', 'lon'), may hold values from -6 to 6
- cell_reach: int32 [512, 4096], P('sec', 'lon'), may hold values from 0 to 65535
- records: bfloat16 [16, 65536, 256], P('lon', 'sec'), may hold values from 0 to 2
- unit_hydro: bfloat16 [16, 65536, 256], P('lon', 'sec'), may hold values from 0.049804688 to 1
- down_basin: int32 [16, 65536], P('lon', 'sec'), may hold values from 0 to 16383
- basin_home: int32 [16, 16384], P('lon'), may hold values from 0 to 16383, as said below
- send_index: int32 [16, 32, 32, 128], P('lon', 'sec'), may hold values from 0 to 2047, as said below
- send_count: int32 [16, 32, 32], P('lon', 'sec'), may hold values from 0 to 128, as said below
Outputs:
- moist_out: float32 [16, 512, 4096], P(None, 'sec', 'lon')
- heat_out: float32 [16, 512, 4096], P(None, 'sec', 'lon')
- record_out: bfloat16 [16, 65536, 256], P('lon', 'sec')
- basin_inflow: float32 [16, 16384, 256], P('lon', 'sec')
Inputs may be any that keep to these rules, and one draw needn't show every extreme that they name: `send_index`: within a longitude group, device s lists each of its 2048 reaches in exactly one used slot; a reach listed in block d drains into a basin whose basin_home lies in d * 512 to (d+1) * 512 - 1. Unused slots hold 0. `send_count`: in every group one owner receives 128 reaches from every device of sec; counts of owners 2 m and 2 m + 1 from one device add up to 128. `basin_home`: each group's row is a permutation.
All inputs are finite; a program needn't handle non-finite values.
Results may differ from a plain program's by a relative error of at most 0.009.
Values may be sent and summed in bfloat16 or wider, within the bound.
A program may use at most 64 MiB of HBM per device.

v0:
```python
import jax
import jax.numpy as jnp
from jax import lax
from jax.sharding import PartitionSpec as P

LATERAL = 0.2


def extended(cells, sides, width):
    for axis, dim in sides:
        count = lax.axis_size(axis)
        ends = count - 1
        head = lax.slice_in_dim(cells, 0, width, axis=dim)
        tail = lax.slice_in_dim(cells, cells.shape[dim] - width, cells.shape[dim], axis=dim)
        cells = jnp.concatenate(
            [
                lax.ppermute(tail, axis, [(i, (i + 1) % count) for i in range(ends)]),
                cells,
                lax.ppermute(head, axis, [((i + 1) % count, i) for i in range(ends)]),
            ],
            axis=dim,
        )
    return cells


def column_solve(conduct, source):
    layer_count = conduct.shape[0]
    flat_zero = jnp.zeros_like(conduct[0])
    links = [0.5 * (conduct[layer] + conduct[layer + 1]) for layer in range(layer_count - 1)]
    above_link = links + [flat_zero]
    below_link = [flat_zero] + links
    prev_ratio = flat_zero
    prev_value = flat_zero
    ratio_list = []
    value_list = []
    for layer in range(layer_count):
        pivot_value = 1.0 + below_link[layer] + above_link[layer] + below_link[layer] * prev_ratio
        prev_ratio = -above_link[layer] / pivot_value
        prev_value = (source[layer] + below_link[layer] * prev_value) / pivot_value
        ratio_list.append(prev_ratio)
        value_list.append(prev_value)
    result = [None] * layer_count
    result[layer_count - 1] = value_list[layer_count - 1]
    for layer in range(layer_count - 2, -1, -1):
        result[layer] = value_list[layer] - ratio_list[layer] * result[layer + 1]
    return jnp.stack(result)


def per_device(
    moisture,
    heat,
    moist_cond,
    heat_cond,
    rain,
    surface_flux,
    cell_reach,
    records,
    unit_hydro,
    down_basin,
    basin_home,
    send_index,
    send_count,
):
    sections = lax.axis_size("sec")
    steps_count = records.shape[2]
    capacity = send_index.shape[3]
    basin_local = basin_home.shape[1] // sections
    rows_left = send_index[0, 0]
    usable = jnp.arange(capacity, dtype=jnp.int32)[None, :] < send_count[0, 0][:, None]
    home_slot = jnp.take(basin_home[0], down_basin[0])
    local_slot = home_slot % basin_local
    slot_ids = jnp.where(usable, jnp.take(local_slot, rows_left), -1)
    stacked = jnp.stack([moisture, heat])
    padded = extended(stacked.astype(jnp.bfloat16), (("lon", 3), ("sec", 2)), 1).astype(
        stacked.dtype
    )
    beside_all = (
        padded[:, :, 2:, 1:-1]
        + padded[:, :, :-2, 1:-1]
        + padded[:, :, 1:-1, 2:]
        + padded[:, :, 1:-1, :-2]
    )
    middle = stacked + LATERAL * (beside_all - 4.0 * stacked)
    moist_rhs = middle[0].at[0].add(rain)
    heat_rhs = middle[1].at[0].add(surface_flux)
    moist_out = column_solve(moist_cond, moist_rhs)
    heat_out = column_solve(heat_cond, heat_rhs)
    layer_last = moist_cond.shape[0] - 1
    runoff = (
        jax.nn.softplus(moist_out[0] - 1.0) * jax.nn.sigmoid(heat_out[0])
        + 0.5 * moist_cond[layer_last] * moist_out[layer_last]
    )
    reach_terms = jax.ops.segment_sum(
        runoff.reshape(-1), cell_reach.reshape(-1), num_segments=records.shape[1] * sections
    )
    reach_runoff = lax.psum_scatter(
        reach_terms.astype(jnp.bfloat16), "sec", scatter_dimension=0, tiled=True
    ).astype(jnp.float32)
    shifted = jnp.concatenate(
        [records[0][:, 1:].astype(jnp.float32), jnp.zeros((records.shape[1], 1), jnp.float32)],
        axis=1,
    )
    record_new = (shifted + reach_runoff[:, None] * unit_hydro[0].astype(jnp.float32)).astype(
        jnp.bfloat16
    )
    arrived, ids_got = (
        lax.all_to_all(record_new[rows_left], "sec", split_axis=0, concat_axis=0, tiled=True),
        lax.all_to_all(slot_ids, "sec", split_axis=0, concat_axis=0, tiled=True),
    )
    onehot = (ids_got.reshape(1, -1) == jnp.arange(basin_local, dtype=jnp.int32)[:, None]).astype(
        jnp.bfloat16
    )
    inflow = jnp.dot(onehot, arrived.reshape(-1, steps_count), preferred_element_type=jnp.float32)
    return (moist_out, heat_out, record_new[None], inflow[None])


def solution(mesh):
    placed = (
        P(None, "sec", "lon"),
        P(None, "sec", "lon"),
        P(None, "sec", "lon"),
        P(None, "sec", "lon"),
        P("sec", "lon"),
        P("sec", "lon"),
        P("sec", "lon"),
        P("lon", "sec", None),
        P("lon", "sec", None),
        P("lon", "sec"),
        P("lon", None),
        P("lon", "sec", None, None),
        P("lon", "sec", None),
    )
    return jax.shard_map(
        per_device,
        mesh=mesh,
        in_specs=placed,
        out_specs=(
            P(None, "sec", "lon"),
            P(None, "sec", "lon"),
            P("lon", "sec", None),
            P("lon", "sec", None),
        ),
        check_vma=False,
    )
```

profile of v0, /device:TPU:1, one launch (start us, length us, event | category | flops | bytes accessed | tf_op | source)
XLA Modules:
  0.0 423.6 jit_solution(12590390196169332106)
XLA Ops:
  7.2 1.1 fusion.8
  8.4 4.0 collective-permute-start
  12.4 1.3 collective-permute-start.1
  13.7 0.7 compare_select_fusion.2
  14.5 0.7 fusion.14
  15.2 0.7 multiply_bitcast_fusion
  15.9 11.8 %gather_fusion = s32[2048]{0:T(1024)S(1)} fusion(s32[16384]{0:T(1024)S(1)} %bitcast.385, s32[2048]{0:T(1024)S(1)} %broadcast_clamp_fusion), kind=kCustom, calls=%fused_computation | custom fusion | bytes 24576 | tf_op jit(solution)/shard_map/jit(_take)/gather | solution.py:70
  27.7 0.3 pad_maximum_fusion.3
  28.0 4.4 %collective-permute-start.2 = (bf16[2,16,1,258]{3,2,1,0:T(2,128)(2,1)S(1)}, bf16[2,16,1,258]{3,2,1,0:T(2,128)(2,1)S(1)}, u32[]{:S(2)}, u32[]{:S(2)}) collective-permute-start(bf16[2,16,1,258]{3,2,1,0:T(2,128)(2,1)S(1)} %get-tuple-element.150), channel_id=1, source_target_pairs={{0,1},{1,2},{2,3},{3,4},{4,5},{5,6},{6,7},{7,8},{8,9},{9,10},{10,1... | collective-permute-start | bytes 49544 | tf_op jit(solution)/shard_map/ppermute | solution.py:17
  32.4 3.0 collective-permute-start.3
  35.5 23.0 %gather_fusion.1 = s32[4096]{0:T(1024)S(1)} fusion(s32[2048]{0:T(1024)S(1)} %add_select_fusion, s32[4096]{0:T(1024)S(1)} %fusion.14), kind=kCustom, calls=%fused_computation.1 | custom fusion | bytes 49152 | tf_op jit(solution)/shard_map/jit(_take)/gather | solution.py:72
  58.5 0.6 maximum_convert_fusion
  59.2 0.5 fusion.7
  59.7 0.3 copy-done.5
  60.1 0.1 fusion.34
  60.8 0.2 fusion.19
  61.3 0.8 constant_dynamic-update-slice_fusion.31
  62.3 0.8 constant_dynamic-update-slice_fusion.15
  63.1 0.3 fusion.12
  63.4 22.0 %scatter_custom_fusion = f32[65536]{0:T(1024)S(1)} fusion(s32[4096]{0:T(1024)S(1)} %bitcast.490, f32[4096]{0:T(1024)S(1)} %fusion.12, f32[]{:T(128)} %constant.102.clone.1), kind=kCustom, calls=%fused_computation.20 | custom fusion | flops 4096 | bytes 262148 | tf_op jit(solution)/shard_map/scatter-add | solution.py:93
  85.4 0.7 convert_element_type.25
  86.1 0.7 compare_select_fusion.1
  86.8 15.6 %all-to-all-start = ((s32[32,1,128]{2,1,0:T(1,128)}), s32[32,1,128]{2,1,0:T(1,128)S(1)}, u32[]{:S(2)}, u32[]{:S(2)}) async-start(s32[32,1,128]{2,1,0:T(1,128)} %compare_select_fusion.1), calls=%async_computation | async-start | bytes 32768 | tf_op jit(solution)/shard_map/all_to_all | solution.py:108
  102.5 0.4 slice.559
  102.9 1.3 dynamic-slice.18
  104.9 182.5 %all-reduce.4.cloned.1.call-done = bf16[65536]{0:T(1024)(128)(2,1)} async-done(((bf16[65536]{0:T(1024)(128)(2,1)}), bf16[65536]{0:T(1024)(128)(2,1)}) %all-reduce.4.cloned.1.call-update) | async-done | bytes 131088
  287.4 0.7 dynamic-slice_convert_fusion
  288.0 1.7 fusion.3
  289.8 17.0 %gather_fusion.2 = bf16[4096,256]{1,0:T(8,128)(2,1)} fusion(bf16[2048,256]{1,0:T(8,128)(2,1)S(1)} %fusion.3, s32[4096]{0:T(1024)S(1)} %fusion.14), kind=kCustom, calls=%fused_computation.2 | custom fusion | bytes 4210688 | tf_op jit(solution)/shard_map/gather | solution.py:107
  306.8 7.5 %all-to-all-start.1 = ((bf16[32,128,256]{2,1,0:T(8,128)(2,1)}), bf16[32,128,256]{2,1,0:T(8,128)(2,1)}, u32[]{:S(2)}, u32[]{:S(2)}) async-start(bf16[32,128,256]{2,1,0:T(8,128)(2,1)} %bitcast.49), calls=%async_computation.1 | async-start | bytes 4194304 | tf_op jit(solution)/shard_map/all_to_all | solution.py:107
  314.9 98.2 %all-to-all-done.1 = bf16[32,128,256]{2,1,0:T(8,128)(2,1)} async-done(((bf16[32,128,256]{2,1,0:T(8,128)(2,1)}), bf16[32,128,256]{2,1,0:T(8,128)(2,1)}, u32[]{:S(2)}, u32[]{:S(2)}) %all-to-all-start.1) | async-done | bytes 2097184 | tf_op jit(solution)/shard_map/all_to_all | solution.py:107
  413.0 3.7 fusion.4
  (137 shorter events, 1.2 us)
Async XLA Ops:
  7.2 8.7 %copy-start = (s32[1,16384]{1,0:T(1,128)S(1)}, s32[1,16384]{1,0:T(1,128)}, u32[]{:S(2)}) copy-start(s32[1,16384]{1,0:T(1,128)} %param.27) | copy-start | bytes 196612
  7.2 280.2 %all-reduce.4.cloned.1.call-start = ((), (), s32[]{:S(2)}) async-start(), calls=%async_computation.2 | async-start | bytes 262144
  8.4 19.3 %collective-permute-start = (bf16[2,16,16,1]{3,2,1,0:T(8,128)(2,1)S(1)}, bf16[2,16,16,1]{3,2,1,0:T(8,128)(2,1)S(1)}, u32[]{:S(2)}, u32[]{:S(2)}) collective-permute-start(bf16[2,16,16,1]{3,2,1,0:T(8,128)(2,1)S(1)} %get-tuple-element.152), channel_id=1, source_target_pairs={{0,32},{32,64},{64,96},{96,128},{128,160},{160,192},{192,224},{224... | collective-permute-start | bytes 3080 | tf_op jit(solution)/shard_map/ppermute | solution.py:17
  12.4 15.3 %collective-permute-start.1 = (bf16[2,16,16,1]{3,2,1,0:T(8,128)(2,1)S(1)}, bf16[2,16,16,1]{3,2,1,0:T(8,128)(2,1)S(1)}, u32[]{:S(2)}, u32[]{:S(2)}) collective-permute-start(bf16[2,16,16,1]{3,2,1,0:T(8,128)(2,1)S(1)} %get-tuple-element.153), channel_id=1, source_target_pairs={{32,0},{64,32},{96,64},{128,96},{160,128},{192,160},{224,192},{256... | collective-permute-start | bytes 3080 | tf_op jit(solution)/shard_map/ppermute | solution.py:19
  15.9 19.5 %copy-start.10 = (s32[1,2048]{1,0:T(1,128)S(1)}, s32[1,2048]{1,0:T(1,128)}, u32[]{:S(2)}) copy-start(s32[1,2048]{1,0:T(1,128)} %param.26) | copy-start | bytes 24580
  15.9 19.5 %copy-start.11 = (s32[16,256]{1,0:T(8,128)S(1)}, s32[16,256]{1,0:T(8,128)}, u32[]{:S(2)}) copy-start(s32[16,256]{1,0:T(8,128)} %param.23) | copy-start | bytes 49156
  28.0 30.5 %collective-permute-start.2 = (bf16[2,16,1,258]{3,2,1,0:T(2,128)(2,1)S(1)}, bf16[2,16,1,258]{3,2,1,0:T(2,128)(2,1)S(1)}, u32[]{:S(2)}, u32[]{:S(2)}) collective-permute-start(bf16[2,16,1,258]{3,2,1,0:T(2,128)(2,1)S(1)} %get-tuple-element.150), channel_id=1, source_target_pairs={{0,1},{1,2},{2,3},{3,4},{4,5},{5,6},{6,7},{7,8},{8,9},{9,10},{10,1... | collective-permute-start | bytes 49544 | tf_op jit(solution)/shard_map/ppermute | solution.py:17
  32.4 26.1 %collective-permute-start.3 = (bf16[2,16,1,258]{3,2,1,0:T(2,128)(2,1)S(1)}, bf16[2,16,1,258]{3,2,1,0:T(2,128)(2,1)S(1)}, u32[]{:S(2)}, u32[]{:S(2)}) collective-permute-start(bf16[2,16,1,258]{3,2,1,0:T(2,128)(2,1)S(1)} %get-tuple-element.151), channel_id=1, source_target_pairs={{1,0},{2,1},{3,2},{4,3},{5,4},{6,5},{7,6},{8,7},{9,8},{10,9},{11,1... | collective-permute-start | bytes 49544 | tf_op jit(solution)/shard_map/ppermute | solution.py:19
  35.4 23.7 %copy-start.2 = (f32[16,16,256]{2,1,0:T(8,128)S(1)}, f32[16,16,256]{2,1,0:T(8,128)}, u32[]{:S(2)}) copy-start(f32[16,16,256]{2,1,0:T(8,128)} %param.18) | copy-start | bytes 786436
  35.5 23.7 %copy-start.3 = (f32[16,16,256]{2,1,0:T(8,128)S(1)}, f32[16,16,256]{2,1,0:T(8,128)}, u32[]{:S(2)}) copy-start(f32[16,16,256]{2,1,0:T(8,128)} %param.17) | copy-start | bytes 786436
  59.1 1.0 copy-start.5
  59.1 0.9 copy-start.8
  59.1 1.1 copy-start.7
  59.7 1.2 copy-start.6
  61.3 24.9 %copy-start.9 = (s32[1,1,32,128]{3,2,1,0:T(8,128)S(1)}, s32[1,1,32,128]{3,2,1,0:T(8,128)}, u32[]{:S(2)}) copy-start(s32[1,1,32,128]{3,2,1,0:T(8,128)} %param.28) | copy-start | bytes 49156
  61.3 24.9 %copy-start.16 = (s32[1,1,32]{2,1,0:T(1,128)S(1)}, s32[1,1,32]{2,1,0:T(1,128)}, u32[]{:S(2)}) copy-start(s32[1,1,32]{2,1,0:T(1,128)} %param.29) | copy-start | bytes 388
  61.3 41.2 %copy-start.4 = (bf16[1,2048,256]{2,1,0:T(8,128)(2,1)S(1)}, bf16[1,2048,256]{2,1,0:T(8,128)(2,1)}, u32[]{:S(2)}) copy-start(bf16[1,2048,256]{2,1,0:T(8,128)(2,1)} %param.24) | copy-start | bytes 3145732
  86.8 220.0 %all-to-all-start = ((s32[32,1,128]{2,1,0:T(1,128)}), s32[32,1,128]{2,1,0:T(1,128)S(1)}, u32[]{:S(2)}, u32[]{:S(2)}) async-start(s32[32,1,128]{2,1,0:T(1,128)} %compare_select_fusion.1), calls=%async_computation | async-start | bytes 32768 | tf_op jit(solution)/shard_map/all_to_all | solution.py:108
  289.8 17.0 %copy-start.1 = (bf16[2048,256]{1,0:T(8,128)(2,1)}, bf16[2048,256]{1,0:T(8,128)(2,1)S(1)}, u32[]{:S(2)}) copy-start(bf16[2048,256]{1,0:T(8,128)(2,1)S(1)} %fusion.3) | copy-start | bytes 3145732
  306.8 7.6 %copy-start.12 = (f32[16,16,256]{2,1,0:T(8,128)S(1)}, f32[16,16,256]{2,1,0:T(8,128)}, u32[]{:S(2)}) copy-start(f32[16,16,256]{2,1,0:T(8,128)} %get-tuple-element.28) | copy-start | bytes 786436
  306.8 7.7 %copy-start.14 = (f32[16,16,256]{2,1,0:T(8,128)S(1)}, f32[16,16,256]{2,1,0:T(8,128)}, u32[]{:S(2)}) copy-start(f32[16,16,256]{2,1,0:T(8,128)} %get-tuple-element.71) | copy-start | bytes 786436
  306.8 106.2 %all-to-all-start.1 = ((bf16[32,128,256]{2,1,0:T(8,128)(2,1)}), bf16[32,128,256]{2,1,0:T(8,128)(2,1)}, u32[]{:S(2)}, u32[]{:S(2)}) async-start(bf16[32,128,256]{2,1,0:T(8,128)(2,1)} %bitcast.49), calls=%async_computation.1 | async-start | bytes 4194304 | tf_op jit(solution)/shard_map/all_to_all | solution.py:107
  314.8 101.9 %copy-start.13 = (f32[16,16,256]{2,1,0:T(8,128)}, f32[16,16,256]{2,1,0:T(8,128)S(1)}, u32[]{:S(2)}) copy-start(f32[16,16,256]{2,1,0:T(8,128)S(1)} %get-tuple-element.146) | copy-start | bytes 786436
  314.8 101.9 %copy-start.15 = (f32[16,16,256]{2,1,0:T(8,128)}, f32[16,16,256]{2,1,0:T(8,128)S(1)}, u32[]{:S(2)}) copy-start(f32[16,16,256]{2,1,0:T(8,128)S(1)} %get-tuple-element.147) | copy-start | bytes 786436
Sparse Core Ops, SparseCore 0:
  86.2 201.0 all-reduce.3
where the time goes:
time: 424 us
  waiting for transfers between devices  281 us (66%)
  local copies, waits for them, and re-layouts  54.8 us (13%)
  starting transfers between devices  35.9 us (8%)
  other arithmetic  32.7 us (8%)
  between operations  15.8 us (4%)
    unnamed x2, waiting for transfers between devices  183 us
    all_to_all x1, waiting for transfers between devices, per_device(): lax.all_to_all(record_new[rows_left], 'sec', split_axis=0, concat_axis=0,...  98.2 us
    gather x1, local copies, waits for them, and re-layouts, per_device(): slot_ids = jnp.where(usable, jnp.take(local_slot, rows_left), -1)  23 us
    scatter-add x1, other arithmetic, per_device(): jax.ops.segment_sum(runoff.reshape(-1), cell_reach.reshape(-1), num_segme...  22 us
    gather x1, local copies, waits for them, and re-layouts, per_device(): record_new[rows_left]  17 us
    all_to_all x1, starting transfers between devices, per_device(): lax.all_to_all(slot_ids, 'sec', split_axis=0, concat_axis=0, tiled=True)  15.6 us
    gather x1, local copies, waits for them, and re-layouts, per_device(): home_slot = jnp.take(basin_home[0], down_basin[0])  11.8 us
  transfers between devices with their start and end apart: 7, of which 2 were waited for; matrix products, arithmetic and copies ran while one was open for 14% of the time, Pallas kernels for 0%

commit v1 on v0

--- a/solution.py
+++ b/solution.py
@@ -4,6 +4,8 @@
 from jax.sharding import PartitionSpec as P
 
 LATERAL = 0.2
+BF = jnp.bfloat16
+F32 = jnp.float32
 
 
 def extended(cells, sides, width):
@@ -46,6 +48,12 @@
     return jnp.stack(result)
 
 
+def marks(ids, count, axis):
+    shape = (count, 1) if axis == 0 else (1, count)
+    ids = ids[None, :] if axis == 0 else ids[:, None]
+    return ids == jnp.arange(count, dtype=jnp.int32).reshape(shape)
+
+
 def per_device(
     moisture,
     heat,
@@ -62,18 +70,34 @@
     send_count,
 ):
     sections = lax.axis_size("sec")
+    reaches = records.shape[1]
     steps_count = records.shape[2]
     capacity = send_index.shape[3]
+    chips = sections // 2
     basin_local = basin_home.shape[1] // sections
-    rows_left = send_index[0, 0]
-    usable = jnp.arange(capacity, dtype=jnp.int32)[None, :] < send_count[0, 0][:, None]
-    home_slot = jnp.take(basin_home[0], down_basin[0])
-    local_slot = home_slot % basin_local
-    slot_ids = jnp.where(usable, jnp.take(local_slot, rows_left), -1)
+    pairs = send_index[0, 0].reshape(chips, 2, capacity)
+    first = send_count[0, 0].reshape(chips, 2)[:, :1]
+    place = jnp.arange(capacity, dtype=jnp.int32)[None, :]
+    packed = jnp.where(place < first, pairs[:, 0], jnp.flip(pairs[:, 1], axis=1)).reshape(-1)
+    table = basin_home[0] % (2 * basin_local)
+    table = jnp.concatenate(
+        [(table // 256).reshape(-1, 128), (table % 256).reshape(-1, 128)], axis=1
+    ).astype(BF)
+    basins = down_basin[0]
+    rows = jnp.dot(
+        marks(basins // 128, table.shape[0], 1).astype(BF), table, preferred_element_type=F32
+    )
+    at = marks(basins % 128, 128, 1)
+    high = jnp.sum(jnp.where(at, rows[:, :128], 0.0), axis=1)
+    low = jnp.sum(jnp.where(at, rows[:, 128:], 0.0), axis=1)
+    pick = marks(packed, reaches, 1).astype(BF)
+    slots = jnp.dot(pick, jnp.stack([high, low], axis=1).astype(BF), preferred_element_type=F32)
+    slots = (slots[:, 0] * 256.0 + slots[:, 1]).astype(jnp.int32)
+    ids_got = lax.all_to_all(
+        slots.reshape(sections, -1), "sec", split_axis=0, concat_axis=0, tiled=True
+    )
     stacked = jnp.stack([moisture, heat])
-    padded = extended(stacked.astype(jnp.bfloat16), (("lon", 3), ("sec", 2)), 1).astype(
-        stacked.dtype
-    )
+    padded = extended(stacked.astype(BF), (("lon", 3), ("sec", 2)), 1).astype(F32)
     beside_all = (
         padded[:, :, 2:, 1:-1]
         + padded[:, :, :-2, 1:-1]
@@ -89,31 +113,32 @@
     runoff = (
         jax.nn.softplus(moist_out[0] - 1.0) * jax.nn.sigmoid(heat_out[0])
         + 0.5 * moist_cond[layer_last] * moist_out[layer_last]
+    ).reshape(-1)
+    cells = cell_reach.reshape(-1)
+    spread = jnp.where(marks(cells // 256, sections * reaches // 256, 0), runoff[None, :], 0.0)
+    terms = jnp.dot(
+        spread.astype(BF), marks(cells % 256, 256, 1).astype(BF), preferred_element_type=F32
     )
-    reach_terms = jax.ops.segment_sum(
-        runoff.reshape(-1), cell_reach.reshape(-1), num_segments=records.shape[1] * sections
+    terms = lax.all_to_all(
+        terms.astype(BF).reshape(sections, -1, 256), "sec", split_axis=0, concat_axis=0, tiled=True
     )
-    reach_runoff = lax.psum_scatter(
-        reach_terms.astype(jnp.bfloat16), "sec", scatter_dimension=0, tiled=True
-    ).astype(jnp.float32)
+    reach_runoff = jnp.sum(terms.astype(F32), axis=0).reshape(-1)
     shifted = jnp.concatenate(
-        [records[0][:, 1:].astype(jnp.float32), jnp.zeros((records.shape[1], 1), jnp.float32)],
-        axis=1,
+        [records[0][:, 1:].astype(F32), jnp.zeros((reaches, 1), F32)], axis=1
     )
-    record_new = (shifted + reach_runoff[:, None] * unit_hydro[0].astype(jnp.float32)).astype(
-        jnp.bfloat16
-    )
-    arrived, ids_got = (
-        lax.all_to_all(record_new[rows_left], "sec", split_axis=0, concat_axis=0, tiled=True),
-        lax.all_to_all(slot_ids, "sec", split_axis=0, concat_axis=0, tiled=True),
-    )
-    onehot = (ids_got.reshape(1, -1) == jnp.arange(basin_local, dtype=jnp.int32)[:, None]).astype(
-        jnp.bfloat16
-    )
-    inflow = jnp.dot(onehot, arrived.reshape(-1, steps_count), preferred_element_type=jnp.float32)
+    record_new = (shifted + reach_runoff[:, None] * unit_hydro[0].astype(F32)).astype(BF)
+    moved = jnp.dot(pick, record_new, preferred_element_type=F32).astype(BF)
+    arrived = lax.all_to_all(
+        moved.reshape(sections, -1, steps_count), "sec", split_axis=0, concat_axis=0, tiled=True
+    ).reshape(-1, steps_count)
+    onehot = marks(ids_got.reshape(-1), 2 * basin_local, 0).astype(BF)
+    sums = jnp.dot(onehot, arrived, preferred_element_type=F32)
+    core = lax.axis_index("sec") % 2
+    halves = sums.reshape(2, basin_local, steps_count)
+    mine = jnp.where(core == 0, halves[0], halves[1])
+    other = jnp.where(core == 0, halves[1], halves[0])
+    inflow = mine + lax.ppermute(other, "sec", [(i, i ^ 1) for i in range(sections)])
     return (moist_out, heat_out, record_new[None], inflow[None])
-
-
 def solution(mesh):
     placed = (
         P(None, "sec", "lon"),

time: 424 us -> 152 us (0.36)
  waiting for transfers between devices: 281 us -> 57.5 us
  local copies, waits for them, and re-layouts: 54.8 us -> 14.8 us
  between operations: 15.8 us -> 1.47 us
  other arithmetic: 32.7 us -> 21.1 us
  matrix products: 3.74 us -> 12.8 us
  starting transfers between devices: 35.9 us -> 42.4 us
    unnamed x2 -> x0, waiting for transfers between devices: 183 us -> none
    gather x3 -> x0, local copies, waits for them, and re-layouts: 51.8 us -> none  [the longest x1 23 us: per_device(): slot_ids = jnp.where(usable, jnp.take(local_slot, rows_left), -1)]
    all_to_all x2 -> x3, waiting for transfers between devices: 98.2 us -> 56.4 us  [the longest x1 39.6 us: per_device(): lax.all_to_all(moved.reshape(sections, -1, steps_count), 'sec', split_axi...]
    scatter-add x1 -> x0, other arithmetic: 22 us -> none  [per_device(): jax.ops.segment_sum(runoff.reshape(-1), cell_reach.reshape(-1), num_segme...]
    unnamed x17 -> x18, other arithmetic: 2.4 us -> 11.6 us
    dot_general x1 -> x5, matrix products: 3.74 us -> 12.8 us  [the longest x1 4.45 us: per_device(): moved = jnp.dot(pick, record_new, preferred_element_type=F32).astype(BF)]
    unnamed x114 -> x101, local copies, waits for them, and re-layouts: 2.44 us -> 11.2 us
    ppermute x2, starting transfers between devices: 4.24 us -> 9.97 us  [extended(): lax.ppermute(head, axis, [((i + 1) % count, i) for i in range(ends)])]
  transfers between devices with their start and end apart: 7 -> 8, of which waited for: 2 -> 4; matrix products, arithmetic and copies ran while one was open for 14% -> 24% of each run, Pallas kernels for 0% -> 0%
where the time goes in v1:
time: 152 us; the launch traced here: 150 us
  waiting for transfers between devices  57.5 us (38%)
  starting transfers between devices  42.4 us (28%)
  other arithmetic  21.1 us (14%)
  local copies, waits for them, and re-layouts  14.8 us (10%)
  matrix products  12.8 us (8%)
    all_to_all x1, waiting for transfers between devices, per_device(): lax.all_to_all(moved.reshape(sections, -1, steps_count), 'sec', split_axi...  39.6 us
    all_to_all x1, starting transfers between devices, per_device(): lax.all_to_all(terms.astype(BF).reshape(sections, -1, 256), 'sec', split_...  13.4 us
    unnamed x18, other arithmetic  11.6 us
    unnamed x101, local copies, waits for them, and re-layouts  11.2 us
    ppermute x2, starting transfers between devices, extended(): lax.ppermute(head, axis, [((i + 1) % count, i) for i in range(ends)])  9.97 us
    all_to_all x1, waiting for transfers between devices, per_device(): lax.all_to_all(terms.astype(BF).reshape(sections, -1, 256), 'sec', split_...  9.36 us
    all_to_all x1, waiting for transfers between devices, per_device(): lax.all_to_all(slots.reshape(sections, -1), 'sec', split_axis=0, concat_a...  7.39 us
    ppermute x2, starting transfers between devices, extended(): lax.ppermute(tail, axis, [(i, (i + 1) % count) for i in range(ends)])  6.59 us
  transfers between devices with their start and end apart: 8, of which 4 were waited for; matrix products, arithmetic and copies ran while one was open for 24% of the time, Pallas kernels for 0%

profile of v1, /device:TPU:1, one launch (start us, length us, event | category | flops | bytes accessed | tf_op | source)
XLA Modules:
  0.0 150.1 jit_solution(17943084737408698774)
XLA Ops:
  0.6 1.1 fusion.23
  1.8 1.3 collective-permute-start.1
  3.1 4.7 %collective-permute-start = (bf16[2,16,16,1]{3,2,1,0:T(8,128)(2,1)S(1)}, bf16[2,16,16,1]{3,2,1,0:T(8,128)(2,1)S(1)}, u32[]{:S(2)}, u32[]{:S(2)}) collective-permute-start(bf16[2,16,16,1]{3,2,1,0:T(8,128)(2,1)S(1)} %get-tuple-element.154), channel_id=1, source_target_pairs={{0,32},{32,64},{64,96},{96,128},{128,160},{160,192},{192,224},{224... | collective-permute-start | bytes 3080 | tf_op jit(solution)/shard_map/ppermute | solution.py:19
  7.8 0.7 copy.22
  9.1 0.7 multiply_bitcast_fusion
  9.9 0.8 fusion.109
  11.3 1.4 reduce.16
  12.7 0.7 add_select_fusion.6
  13.4 0.9 fusion.25
  15.5 8.7 %collective-permute-start.3 = (bf16[2,16,1,258]{3,2,1,0:T(2,128)(2,1)S(1)}, bf16[2,16,1,258]{3,2,1,0:T(2,128)(2,1)S(1)}, u32[]{:S(2)}, u32[]{:S(2)}) collective-permute-start(bf16[2,16,1,258]{3,2,1,0:T(2,128)(2,1)S(1)} %get-tuple-element.153), channel_id=1, source_target_pairs={{1,0},{2,1},{3,2},{4,3},{5,4},{6,5},{7,6},{8,7},{9,8},{10,9},{11,1... | collective-permute-start | bytes 49544 | tf_op jit(solution)/shard_map/ppermute | solution.py:21
  24.1 1.9 %collective-permute-start.2 = (bf16[2,16,1,258]{3,2,1,0:T(2,128)(2,1)S(1)}, bf16[2,16,1,258]{3,2,1,0:T(2,128)(2,1)S(1)}, u32[]{:S(2)}, u32[]{:S(2)}) collective-permute-start(bf16[2,16,1,258]{3,2,1,0:T(2,128)(2,1)S(1)} %get-tuple-element.152), channel_id=1, source_target_pairs={{0,1},{1,2},{2,3},{3,4},{4,5},{5,6},{6,7},{7,8},{8,9},{9,10},{10,1... | collective-permute-start | bytes 49544 | tf_op jit(solution)/shard_map/ppermute | solution.py:19
  26.2 1.1 collective-permute-done.2
  29.2 0.8 constant_dynamic-update-slice_fusion.31
  30.5 0.8 constant_dynamic-update-slice_fusion.15
  32.2 1.8 %fusion.15 = bf16[32,8,256]{2,1,0:T(8,128)(2,1)} fusion(s32[4096]{0:T(1024)S(1)} %copy-done.9, bf16[4096]{0:T(1024)(128)(2,1)S(1)} %fusion.33, s32[4096]{0:T(1024)S(1)} %get-tuple-element.160), kind=kOutput, calls=%fused_computation.21 | convolution fusion | flops 540082176 | bytes 172032 | tf_op jit(solution)/shard_map/dot_general | solution.py:119
  34.0 13.4 %all-to-all-start = ((bf16[32,8,256]{2,1,0:T(8,128)(2,1)}), bf16[32,8,256]{2,1,0:T(8,128)(2,1)S(1)}, u32[]{:S(2)}, u32[]{:S(2)}) async-start(bf16[32,8,256]{2,1,0:T(8,128)(2,1)} %fusion.15), calls=%async_computation | async-start | bytes 262144 | tf_op jit(solution)/shard_map/all_to_all | solution.py:122
  47.6 1.7 %slice.593 = bf16[2048,255]{1,0:T(8,128)(2,1)S(1)} slice(bf16[2048,256]{1,0:T(8,128)(2,1)} %bitcast.391), slice={[0:2048], [1:256]} | slice | bytes 2088960 | tf_op jit(solution)/shard_map/slice | solution.py:127
  49.3 3.2 %fusion.1 = f32[2048,2]{0,1:T(2,128)S(1)} fusion(s32[2048]{0:T(1024)S(1)} %select_bitcast_fusion, bf16[2048,1]{0,1:T(2,128)(2,1)S(1)} %stack.25, bf16[2048,1]{0,1:T(2,128)(2,1)S(1)} %stack.24), kind=kOutput, calls=%fused_computation.2 | convolution fusion | flops 20987904 | bytes 32768 | tf_op jit(solution)/shard_map/dot_general | solution.py:94
  52.6 0.7 convert_element_type.57
  53.8 9.4 %all-to-all-done = bf16[32,8,256]{2,1,0:T(8,128)(2,1)S(1)} async-done(((bf16[32,8,256]{2,1,0:T(8,128)(2,1)}), bf16[32,8,256]{2,1,0:T(8,128)(2,1)S(1)}, u32[]{:S(2)}, u32[]{:S(2)}) %all-to-all-start) | async-done | bytes 131104 | tf_op jit(solution)/shard_map/all_to_all | solution.py:122
  63.2 5.0 %all-to-all-start.1 = ((s32[32,1,64]{2,1,0:T(1,128)}), s32[32,1,64]{2,1,0:T(1,128)S(1)}, u32[]{:S(2)}, u32[]{:S(2)}) async-start(s32[32,1,64]{2,1,0:T(1,128)} %bitcast.46), calls=%async_computation.1 | async-start | bytes 32768 | tf_op jit(solution)/shard_map/all_to_all | solution.py:96
  68.3 4.5 %fusion.7 = bf16[2048,256]{1,0:T(8,128)(2,1)} fusion(s32[2048]{0:T(1024)S(1)} %select_bitcast_fusion, bf16[1,2048,256]{2,1,0:T(8,128)(2,1)S(1)} %copy-done, f32[2048]{0:T(1024)S(1)} %bitcast.489, bf16[2048,255]{1,0:T(8,128)(2,1)S(1)} %slice.593), kind=kOutput, calls=%fused_computation.12 | convolution fusion | flops 2154823680 | bytes 3158016 | tf_op jit(solution)/shard_map/dot_general | solution.py:130
  72.7 7.4 %all-to-all-done.1 = s32[32,1,64]{2,1,0:T(1,128)S(1)} async-done(((s32[32,1,64]{2,1,0:T(1,128)}), s32[32,1,64]{2,1,0:T(1,128)S(1)}, u32[]{:S(2)}, u32[]{:S(2)}) %all-to-all-start.1) | async-done | bytes 8224 | tf_op jit(solution)/shard_map/all_to_all | solution.py:96
  80.1 4.9 %all-to-all-start.2 = ((bf16[32,64,256]{2,1,0:T(8,128)(2,1)}), bf16[32,64,256]{2,1,0:T(8,128)(2,1)S(1)}, u32[]{:S(2)}, u32[]{:S(2)}) async-start(bf16[32,64,256]{2,1,0:T(8,128)(2,1)} %bitcast.392), calls=%async_computation.2 | async-start | bytes 2097152 | tf_op jit(solution)/shard_map/all_to_all | solution.py:131
  100.3 0.7 reduce.17
  101.1 39.6 %all-to-all-done.2 = bf16[32,64,256]{2,1,0:T(8,128)(2,1)S(1)} async-done(((bf16[32,64,256]{2,1,0:T(8,128)(2,1)}), bf16[32,64,256]{2,1,0:T(8,128)(2,1)S(1)}, u32[]{:S(2)}, u32[]{:S(2)}) %all-to-all-start.2) | async-done | bytes 1048608 | tf_op jit(solution)/shard_map/all_to_all | solution.py:131
  140.8 1.0 copy-done.4
  141.7 2.7 %fusion.4 = f32[1024,256]{1,0:T(8,128)S(1)} fusion(bf16[2048,256]{1,0:T(8,128)(2,1)} %bitcast.393, s32[2048]{0:T(1024)S(1)} %eq.112), kind=kOutput, calls=%fused_computation.6 | convolution fusion | flops 1075838976 | bytes 2105344 | tf_op jit(solution)/shard_map/dot_general | solution.py:135
  144.5 2.5 %collective-permute-start.4 = (f32[512,256]{1,0:T(8,128)S(1)}, f32[512,256]{1,0:T(8,128)S(1)}, u32[]{:S(2)}, u32[]{:S(2)}) collective-permute-start(f32[512,256]{1,0:T(8,128)S(1)} %slice_select_fusion.2), channel_id=1, source_target_pairs={{0,1},{1,0},{2,3},{3,2},{4,5},{5,4},{6,7},{7,6},{8,9},{9,8},{10,11... | collective-permute-start | bytes 1572872 | tf_op jit(solution)/shard_map/ppermute | solution.py:140
  147.0 0.7 constant_dynamic-update-slice_fusion.16
  147.7 1.5 fusion.81
  149.2 0.9 add_bitcast_fusion
  (137 shorter events, 21.7 us)
Async XLA Ops:
  1.8 13.4 %collective-permute-start.1 = (bf16[2,16,16,1]{3,2,1,0:T(8,128)(2,1)S(1)}, bf16[2,16,16,1]{3,2,1,0:T(8,128)(2,1)S(1)}, u32[]{:S(2)}, u32[]{:S(2)}) collective-permute-start(bf16[2,16,16,1]{3,2,1,0:T(8,128)(2,1)S(1)} %get-tuple-element.155), channel_id=1, source_target_pairs={{32,0},{64,32},{96,64},{128,96},{160,128},{192,160},{224,192},{256... | collective-permute-start | bytes 3080 | tf_op jit(solution)/shard_map/ppermute | solution.py:21
  3.1 12.1 %collective-permute-start = (bf16[2,16,16,1]{3,2,1,0:T(8,128)(2,1)S(1)}, bf16[2,16,16,1]{3,2,1,0:T(8,128)(2,1)S(1)}, u32[]{:S(2)}, u32[]{:S(2)}) collective-permute-start(bf16[2,16,16,1]{3,2,1,0:T(8,128)(2,1)S(1)} %get-tuple-element.154), channel_id=1, source_target_pairs={{0,32},{32,64},{64,96},{96,128},{128,160},{160,192},{192,224},{224... | collective-permute-start | bytes 3080 | tf_op jit(solution)/shard_map/ppermute | solution.py:19
  14.4 13.5 %copy-start.2 = (f32[16,16,256]{2,1,0:T(8,128)S(1)}, f32[16,16,256]{2,1,0:T(8,128)}, u32[]{:S(2)}) copy-start(f32[16,16,256]{2,1,0:T(8,128)} %param.18) | copy-start | bytes 786436
  14.4 13.5 %copy-start.3 = (f32[16,16,256]{2,1,0:T(8,128)S(1)}, f32[16,16,256]{2,1,0:T(8,128)}, u32[]{:S(2)}) copy-start(f32[16,16,256]{2,1,0:T(8,128)} %param.17) | copy-start | bytes 786436
  15.5 10.7 %collective-permute-start.3 = (bf16[2,16,1,258]{3,2,1,0:T(2,128)(2,1)S(1)}, bf16[2,16,1,258]{3,2,1,0:T(2,128)(2,1)S(1)}, u32[]{:S(2)}, u32[]{:S(2)}) collective-permute-start(bf16[2,16,1,258]{3,2,1,0:T(2,128)(2,1)S(1)} %get-tuple-element.153), channel_id=1, source_target_pairs={{1,0},{2,1},{3,2},{4,3},{5,4},{6,5},{7,6},{8,7},{9,8},{10,9},{11,1... | collective-permute-start | bytes 49544 | tf_op jit(solution)/shard_map/ppermute | solution.py:21
  24.1 3.1 %collective-permute-start.2 = (bf16[2,16,1,258]{3,2,1,0:T(2,128)(2,1)S(1)}, bf16[2,16,1,258]{3,2,1,0:T(2,128)(2,1)S(1)}, u32[]{:S(2)}, u32[]{:S(2)}) collective-permute-start(bf16[2,16,1,258]{3,2,1,0:T(2,128)(2,1)S(1)} %get-tuple-element.152), channel_id=1, source_target_pairs={{0,1},{1,2},{2,3},{3,4},{4,5},{5,6},{6,7},{7,8},{8,9},{9,10},{10,1... | collective-permute-start | bytes 49544 | tf_op jit(solution)/shard_map/ppermute | solution.py:19
  27.9 1.0 copy-start.5
  27.9 0.9 copy-start.8
  27.9 1.1 copy-start.7
  27.9 1.1 copy-start.6
  29.9 2.2 %copy-start.9 = (s32[4096]{0:T(1024)S(1)}, s32[4096]{0:T(1024)}, u32[]{:S(2)}) copy-start(s32[4096]{0:T(1024)} %get-tuple-element.161) | copy-start | bytes 49156
  34.0 29.2 %all-to-all-start = ((bf16[32,8,256]{2,1,0:T(8,128)(2,1)}), bf16[32,8,256]{2,1,0:T(8,128)(2,1)S(1)}, u32[]{:S(2)}, u32[]{:S(2)}) async-start(bf16[32,8,256]{2,1,0:T(8,128)(2,1)} %fusion.15), calls=%async_computation | async-start | bytes 262144 | tf_op jit(solution)/shard_map/all_to_all | solution.py:122
  49.3 19.0 %copy-start = (bf16[1,2048,256]{2,1,0:T(8,128)(2,1)S(1)}, bf16[1,2048,256]{2,1,0:T(8,128)(2,1)}, u32[]{:S(2)}) copy-start(bf16[1,2048,256]{2,1,0:T(8,128)(2,1)} %param.25) | copy-start | bytes 3145732
  63.2 16.9 %all-to-all-start.1 = ((s32[32,1,64]{2,1,0:T(1,128)}), s32[32,1,64]{2,1,0:T(1,128)S(1)}, u32[]{:S(2)}, u32[]{:S(2)}) async-start(s32[32,1,64]{2,1,0:T(1,128)} %bitcast.46), calls=%async_computation.1 | async-start | bytes 32768 | tf_op jit(solution)/shard_map/all_to_all | solution.py:96
  80.1 60.6 %all-to-all-start.2 = ((bf16[32,64,256]{2,1,0:T(8,128)(2,1)}), bf16[32,64,256]{2,1,0:T(8,128)(2,1)S(1)}, u32[]{:S(2)}, u32[]{:S(2)}) async-start(bf16[32,64,256]{2,1,0:T(8,128)(2,1)} %bitcast.392), calls=%async_computation.2 | async-start | bytes 2097152 | tf_op jit(solution)/shard_map/all_to_all | solution.py:131
  140.7 1.0 copy-start.4
  144.4 3.3 %copy-start.1 = (bf16[1,2048,256]{2,1,0:T(8,128)(2,1)S(1)}, bf16[1,2048,256]{2,1,0:T(8,128)(2,1)}, u32[]{:S(2)}) copy-start(bf16[1,2048,256]{2,1,0:T(8,128)(2,1)} %param.25) | copy-start | bytes 3145732
  144.5 4.7 %collective-permute-start.4 = (f32[512,256]{1,0:T(8,128)S(1)}, f32[512,256]{1,0:T(8,128)S(1)}, u32[]{:S(2)}, u32[]{:S(2)}) collective-permute-start(f32[512,256]{1,0:T(8,128)S(1)} %slice_select_fusion.2), channel_id=1, source_target_pairs={{0,1},{1,0},{2,3},{3,2},{4,5},{5,4},{6,7},{7,6},{8,9},{9,8},{10,11... | collective-permute-start | bytes 1572872 | tf_op jit(solution)/shard_map/ppermute | solution.py:140

commit v2 on v0

v2 whole, which is shorter than its diff:
```python
import jax
import jax.numpy as jnp
from jax import lax
from jax.experimental import pallas as pl
from jax.experimental.pallas import tpu as pltpu
from jax.sharding import PartitionSpec as P

LATERAL = 0.2
BF = jnp.bfloat16
F32 = jnp.float32
I32 = jnp.int32
NT = (((1,), (1,)), ((), ()))


def iota(shape, axis):
    return lax.broadcasted_iota(I32, shape, axis)


def ones_where(mask):
    return jnp.where(mask, 1.0, 0.0).astype(BF)


def dot(a, b):
    return jnp.dot(a, b, preferred_element_type=F32)


def dot_nt(a, b):
    return lax.dot_general(a, b, NT, preferred_element_type=F32)


def column(block, lane):
    shape = block.shape
    return jnp.sum(jnp.where(iota(shape, 1) == lane, block, 0.0), axis=1, keepdims=True)


def kernel(
    moist,
    heat,
    moist_cond,
    heat_cond,
    rain,
    flux,
    cells,
    records,
    hydro,
    basins,
    homes,
    send_index,
    send_count,
    moist_out,
    heat_out,
    record_out,
    inflow,
    base,
    inv,
    back,
    ratio,
    row_out,
    row_in,
    col_out,
    col_in,
    cells_in,
    value_out,
    value_in,
    hi,
    lo,
    value,
    spread,
    marks,
    terms_out,
    terms_in,
    places,
    picks,
    slots,
    ids_out,
    ids_in,
    shifted,
    hydro_at,
    rows_out,
    rows_in,
    chosen,
    sums,
    sums_in,
    halo_send,
    halo_recv,
    pair_send,
    pair_recv,
    terms_send,
    terms_recv,
    ids_send,
    ids_recv,
    rows_send,
    rows_recv,
):
    layers, lats, width = moist.shape
    chips = rows_out.shape[0]
    cap = rows_out.shape[1]
    steps = rows_out.shape[2]
    reaches = records.shape[0]
    lon, sec = lax.axis_index("lon"), lax.axis_index("sec")
    n_lon, n_sec = lax.axis_size("lon"), lax.axis_size("sec")
    chip, core = sec // 2, sec % 2
    partner = chip * 2 + 1 - core
    up, down = (sec + n_sec - 1) % n_sec, (sec + 1) % n_sec
    left, right = (lon + n_lon - 1) % n_lon, (lon + 1) % n_lon

    def ahead(k):
        return chips // 2 + ((k + 1) // 2) * (2 * (k % 2) - 1)

    def target(k):
        return (chip + ahead(k)) % chips

    def copy(src, dst, send, recv, **where):
        return pltpu.make_async_remote_copy(
            src_ref=src, dst_ref=dst, send_sem=send, recv_sem=recv, device_id=where
        )

    barrier = pltpu.get_barrier_semaphore()

    def greet(k, _):
        pl.semaphore_signal(barrier, inc=1, device_id={"sec": target(k) * 2 + core})
        return 0

    lax.fori_loop(0, chips - 1, greet, 0)
    for peer in ({"sec": up}, {"sec": down}, {"lon": left}, {"lon": right}):
        pl.semaphore_signal(barrier, inc=1, device_id=peer)

    lane_e = iota((lats, 128), 1)
    first = jnp.zeros((lats, 128), F32)
    last = jnp.zeros((lats, 128), F32)
    for f, field in enumerate((moist, heat)):
        row_out[0, f] = field[:, 0, :].astype(BF)
        row_out[1, f] = field[:, lats - 1, :].astype(BF)
        for layer in range(layers):
            first = jnp.where(lane_e == f * layers + layer, field[layer, :, 0:1], first)
            last = jnp.where(
                lane_e == f * layers + layer, field[layer, :, width - 1 : width], last
            )
    col_out[0] = first
    col_out[1] = last

    row_at, lane_at = iota((lats, width), 0), iota((lats, width), 1)
    for f, (field, cond, extra) in enumerate(
        ((moist, moist_cond, rain), (heat, heat_cond, flux))
    ):
        for layer in range(layers):
            x = field[layer]
            near = (
                jnp.where(row_at == 0, 0.0, pltpu.roll(x, 1, 0))
                + jnp.where(row_at == lats - 1, 0.0, pltpu.roll(x, lats - 1, 0))
                + jnp.where(lane_at == 0, 0.0, pltpu.roll(x, 1, 1))
                + jnp.where(lane_at == width - 1, 0.0, pltpu.roll(x, width - 1, 1))
            )
            x = x + LATERAL * (near - 4.0 * x)
            base[f, layer] = x + extra[...] if layer == 0 else x
        prev = jnp.zeros((lats, width), F32)
        below = jnp.zeros((lats, width), F32)
        for layer in range(layers):
            if layer + 1 < layers:
                above = 0.5 * (cond[layer] + cond[layer + 1])
            else:
                above = jnp.zeros((lats, width), F32)
            part = 1.0 / (1.0 + below + above + below * prev)
            prev = -above * part
            inv[f, layer] = part
            back[f, layer] = below * part
            ratio[f, layer] = prev
            below = above

    def cell_marks(at, where):
        reach = where[...]
        rows = pl.ds(at, lats)
        hi[rows] = jnp.where(
            (reach // reaches) % 2 == core,
            (reach // (2 * reaches)) * (reaches // 256) + (reach // 256) % (reaches // 256),
            -1,
        )
        lo[rows] = reach % 256

        def mark(r, _):
            lanes = pl.ds(pl.multiple_of(r * width, width), width)
            marks[:, lanes] = ones_where(lo[pl.ds(r, 1), :] == iota((256, width), 0))
            return 0

        lax.fori_loop(at, at + lats, mark, 0)

    cell_marks(0, cells)

    eye = ones_where(iota((128, 128), 0) == iota((128, 128), 1))
    flip = ones_where(iota((128, 128), 0) + iota((128, 128), 1) == 127)
    basin = basins[...]
    basin_cols = dot_nt(
        eye, jnp.concatenate([basin // 128, basin % 128], axis=0).astype(F32).astype(BF)
    )
    home = homes[...] % (2 * inflow.shape[0])
    table = jnp.concatenate([home // 256, home % 256], axis=1).astype(F32).astype(BF)
    groups = reaches // 128

    def look(m, _):
        found = dot(ones_where(column(basin_cols, m).astype(I32) == iota((128, 128), 1)), table)
        at = column(basin_cols, groups + m).astype(I32) == iota((128, 128), 1)
        high = jnp.sum(jnp.where(at, found[:, :128], 0.0), axis=1, keepdims=True)
        low = jnp.sum(jnp.where(at, found[:, 128:], 0.0), axis=1, keepdims=True)
        lane = iota((128, 128), 1)
        places[pl.ds(pl.multiple_of(m * 128, 128), 128), :] = jnp.where(
            lane == 0, high, jnp.where(lane == 1, low, 0.0)
        ).astype(BF)
        return 0

    lax.fori_loop(0, groups, look, 0)

    even = send_index[pl.ds(0, chips, stride=2), :]
    odd = send_index[pl.ds(1, chips, stride=2), :]

    def halves(x):
        return jnp.concatenate([x // 256, x % 256], axis=0).astype(F32).astype(BF)

    pick_even = ones_where(
        iota((2 * chips, 2 * chips), 0) == 2 * (iota((2 * chips, 2 * chips), 1) % chips)
    )
    counts = dot(
        jnp.broadcast_to(send_count[...], (8, 2 * chips)).astype(F32).astype(BF), pick_even
    )
    picks[...] = jnp.where(
        iota((cap, 2 * chips), 0).astype(F32) < counts[0:1, :],
        dot_nt(eye, halves(even)),
        dot_nt(flip, halves(odd)),
    )

    pl.semaphore_wait(barrier, chips - 1 + 4)

    halo = [
        copy(row_out.at[0], row_in.at[1], halo_send.at[0], halo_recv.at[1], sec=up),
        copy(row_out.at[1], row_in.at[0], halo_send.at[1], halo_recv.at[0], sec=down),
        copy(col_out.at[0], col_in.at[1], halo_send.at[2], halo_recv.at[3], lon=left),
        copy(col_out.at[1], col_in.at[0], halo_send.at[3], halo_recv.at[2], lon=right),
    ]
    reach_pair = copy(cells, cells_in, pair_send.at[0], pair_recv.at[0], sec=partner)
    for one in halo:
        one.start()
    reach_pair.start()
    reach_pair.wait()
    cell_marks(lats, cells_in)
    for one in halo:
        one.wait()

    has_up = jnp.where(sec > 0, LATERAL, 0.0)
    has_down = jnp.where(sec < n_sec - 1, LATERAL, 0.0)
    has_left = jnp.where(lon > 0, LATERAL, 0.0)
    has_right = jnp.where(lon < n_lon - 1, LATERAL, 0.0)
    runoff = None
    surface = []
    for f, out in enumerate((moist_out, heat_out)):
        above_rows = row_in[0, f].astype(F32) * has_up
        below_rows = row_in[1, f].astype(F32) * has_down
        first = col_in[0] * has_left
        last = col_in[1] * has_right
        held = []
        prev = jnp.zeros((lats, width), F32)
        for layer in range(layers):
            lane = f * layers + layer
            source = (
                base[f, layer]
                + jnp.where(row_at == 0, above_rows[layer : layer + 1, :], 0.0)
                + jnp.where(row_at == lats - 1, below_rows[layer : layer + 1, :], 0.0)
                + jnp.where(lane_at == 0, first[:, lane : lane + 1], 0.0)
                + jnp.where(lane_at == width - 1, last[:, lane : lane + 1], 0.0)
            )
            prev = source * inv[f, layer] + back[f, layer] * prev
            held.append(prev)
        x = held[-1]
        out[layers - 1] = x
        if f == 0:
            runoff = 0.5 * moist_cond[layers - 1] * x
        for layer in range(layers - 2, -1, -1):
            x = held[layer] - ratio[f, layer] * x
            out[layer] = x
        surface.append(x)
    wet = surface[0] - 1.0
    softplus = jnp.maximum(wet, 0.0) + jnp.log1p(jnp.exp(-jnp.abs(wet)))
    runoff = softplus * jax.nn.sigmoid(surface[1]) + runoff
    value_out[...] = runoff.astype(BF)
    value_pair = copy(value_out, value_in, pair_send.at[1], pair_recv.at[1], sec=partner)
    value_pair.start()
    value[pl.ds(0, lats)] = runoff

    def spread_rows(r, _):
        lanes = pl.ds(pl.multiple_of(r * width, width), width)
        at = hi[pl.ds(r, 1), :] == iota((spread.shape[0], width), 0)
        spread[:, lanes] = jnp.where(at, value[pl.ds(r, 1), :], 0.0).astype(BF)
        return 0

    lax.fori_loop(0, lats, spread_rows, 0)
    half = lats * width
    terms = dot_nt(spread[:, :half], marks[:, :half])
    value_pair.wait()
    value[pl.ds(lats, lats)] = value_in[...].astype(F32)
    lax.fori_loop(lats, 2 * lats, spread_rows, 0)
    terms = terms + dot_nt(spread[:, half:], marks[:, half:])
    terms_out[...] = terms.astype(BF).reshape(terms_out.shape)

    def terms_copy(k):
        return copy(
            terms_out.at[target(k)],
            terms_in.at[k],
            terms_send.at[k],
            terms_recv.at[k],
            sec=target(k) * 2 + core,
        )

    def terms_start(k, _):
        terms_copy(k).start()
        return 0

    lax.fori_loop(0, chips - 1, terms_start, 0)
    terms_in[chips - 1] = terms_out[chip]

    lane_s = iota((cap, steps), 1)

    def pack(m, ids):
        at = column(picks[...], m) * 256.0 + column(picks[...], chips + m)
        pick = ones_where(at.astype(I32) == iota((cap, reaches), 1))
        place = dot(pick, places[...])
        hydro_at[m] = dot(pick, hydro[...])
        moved = pltpu.roll(dot(pick, records[...]), steps - 1, 1)
        shifted[m] = jnp.where(lane_s == steps - 1, 0.0, moved)
        place = column(place, 0) * 256.0 + column(place, 1)
        return jnp.where(iota((cap, 128), 1) == m, place, ids)

    ids = lax.fori_loop(0, chips, pack, jnp.zeros((cap, 128), F32))
    slots[...] = ids.T.astype(I32)

    def ids_copy(k):
        return copy(
            ids_out.at[target(k)],
            ids_in.at[k],
            ids_send.at[k],
            ids_recv.at[k],
            sec=target(k) * 2 + core,
        )

    def ids_fill(m, _):
        ids_out[m] = jnp.broadcast_to(slots[pl.ds(m, 1), :], (8, 128))
        return 0

    def ids_start(k, _):
        ids_copy(k).start()
        return 0

    lax.fori_loop(0, chips, ids_fill, 0)
    lax.fori_loop(0, chips - 1, ids_start, 0)
    ids_in[chips - 1] = ids_out[chip]

    def terms_wait(k, _):
        terms_copy(k).wait()
        return 0

    lax.fori_loop(0, chips - 1, terms_wait, 0)
    reach_runoff = terms_in[0].astype(F32)
    for k in range(1, chips):
        reach_runoff = reach_runoff + terms_in[k].astype(F32)
    coarse = reach_runoff.astype(BF)
    fine = (reach_runoff - coarse.astype(F32)).astype(BF)
    both = jnp.concatenate([coarse.astype(F32), fine.astype(F32)], axis=0).astype(BF)
    parts = both.shape[0]

    def make_rows(m):
        octet = column(picks[...], m).astype(I32)
        found = dot(ones_where(octet == iota((cap, parts), 1) % (parts // 2)), both)
        at = column(picks[...], chips + m).astype(I32) == iota((cap, 256), 1)
        scale = jnp.sum(jnp.where(at, found, 0.0), axis=1, keepdims=True)
        return (shifted[m] + scale * hydro_at[m]).astype(BF)

    def rows_copy(k):
        return copy(
            rows_out.at[k],
            rows_in.at[k],
            rows_send.at[k],
            rows_recv.at[k],
            sec=target(k) * 2 + core,
        )

    def rows_start(k, _):
        rows_out[k] = make_rows(target(k))
        rows_copy(k).start()
        return 0

    lax.fori_loop(0, chips - 1, rows_start, 0)
    rows_in[chips - 1] = make_rows(chip)

    diagonal = iota((256, 256), 0) == iota((256, 256), 1)
    lane_w = iota((256, steps), 1)
    for j in range(reaches // 256):
        scale = jnp.sum(
            jnp.where(diagonal, reach_runoff[j : j + 1, :], 0.0), axis=1, keepdims=True
        )
        rows = pl.ds(j * 256, 256)
        moved = pltpu.roll(records[rows, :].astype(F32), steps - 1, 1)
        moved = jnp.where(lane_w == steps - 1, 0.0, moved)
        record_out[rows, :] = (moved + scale * hydro[rows, :].astype(F32)).astype(BF)

    def ids_wait(k, _):
        ids_copy(k).wait()
        return 0

    lax.fori_loop(0, chips - 1, ids_wait, 0)

    def choose(i, _):
        got = jnp.concatenate([ids_in[2 * i][0:1, :], ids_in[2 * i + 1][0:1, :]], axis=1)
        chosen[i] = ones_where(got == iota((sums.shape[0], 2 * cap), 0))
        return 0

    lax.fori_loop(0, chips // 2, choose, 0)

    def gain(i):
        pair = rows_in[pl.ds(2 * i, 2)].reshape(2 * cap, steps)
        return dot(chosen[i], pair)

    rows_copy(0).wait()
    rows_copy(1).wait()
    sums[...] = gain(0)

    def add(i, _):
        rows_copy(2 * i).wait()
        rows_copy(2 * i + 1).wait()
        sums[...] += gain(i)
        return 0

    lax.fori_loop(1, chips // 2 - 1, add, 0)
    rows_copy(chips - 2).wait()
    sums[...] += gain(chips // 2 - 1)
    mine = inflow.shape[0]
    swap = copy(
        sums.at[pl.ds(pl.multiple_of((1 - core) * mine, mine), mine)],
        sums_in,
        pair_send.at[2],
        pair_recv.at[2],
        sec=partner,
    )
    swap.start()
    swap.wait()
    inflow[...] = sums[pl.ds(pl.multiple_of(core * mine, mine), mine), :] + sums_in[...]


def per_device(
    moisture,
    heat,
    moist_cond,
    heat_cond,
    rain,
    surface_flux,
    cell_reach,
    records,
    unit_hydro,
    down_basin,
    basin_home,
    send_index,
    send_count,
):
    sections = lax.axis_size("sec")
    chips = sections // 2
    layers, lats, width = moisture.shape
    reaches, steps = records.shape[1:]
    cap = send_index.shape[3]
    mine = basin_home.shape[1] // sections
    field = (2, layers, lats, width)
    octets = reaches // 256
    vmem = pltpu.VMEM
    sem = pltpu.SemaphoreType.DMA
    out = pl.pallas_call(
        kernel,
        out_shape=(
            jax.ShapeDtypeStruct(moisture.shape, F32),
            jax.ShapeDtypeStruct(heat.shape, F32),
            jax.ShapeDtypeStruct((reaches, steps), BF),
            jax.ShapeDtypeStruct((mine, steps), F32),
        ),
        in_specs=[pl.BlockSpec(memory_space=vmem)] * 13,
        out_specs=tuple([pl.BlockSpec(memory_space=vmem)] * 4),
        scratch_shapes=[
            vmem(field, F32),
            vmem(field, F32),
            vmem(field, F32),
            vmem(field, F32),
            vmem((2, 2, layers, width), BF),
            vmem((2, 2, layers, width), BF),
            vmem((2, lats, 128), F32),
            vmem((2, lats, 128), F32),
            vmem((lats, width), I32),
            vmem((lats, width), BF),
            vmem((lats, width), BF),
            vmem((2 * lats, width), I32),
            vmem((2 * lats, width), I32),
            vmem((2 * lats, width), F32),
            vmem((chips * octets, 2 * lats * width), BF),
            vmem((256, 2 * lats * width), BF),
            vmem((chips, octets, 256), BF),
            vmem((chips, octets, 256), BF),
            vmem((reaches, 128), BF),
            vmem((cap, 2 * chips), F32),
            vmem((128, cap), I32),
            vmem((chips, 8, 128), I32),
            vmem((chips, 8, 128), I32),
            vmem((chips, cap, steps), F32),
            vmem((chips, cap, steps), F32),
            vmem((chips, cap, steps), BF),
            vmem((chips, cap, steps), BF),
            vmem((chips // 2, 2 * mine, 2 * cap), BF),
            vmem((2 * mine, steps), F32),
            vmem((mine, steps), F32),
            sem((4,)),
            sem((4,)),
            sem((3,)),
            sem((3,)),
            sem((chips,)),
            sem((chips,)),
            sem((chips,)),
            sem((chips,)),
            sem((chips,)),
            sem((chips,)),
        ],
        compiler_params=pltpu.CompilerParams(
            collective_id=0, has_side_effects=True, vmem_limit_bytes=60 * 1024 * 1024
        ),
    )(
        moisture,
        heat,
        moist_cond,
        heat_cond,
        rain,
        surface_flux,
        cell_reach,
        records[0],
        unit_hydro[0],
        down_basin.reshape(reaches // 128, 128),
        basin_home.reshape(-1, 128),
        send_index[0, 0],
        send_count[0],
    )
    return out[0], out[1], out[2][None], out[3][None]


def solution(mesh):
    placed = (
        P(None, "sec", "lon"),
        P(None, "sec", "lon"),
        P(None, "sec", "lon"),
        P(None, "sec", "lon"),
        P("sec", "lon"),
        P("sec", "lon"),
        P("sec", "lon"),
        P("lon", "sec", None),
        P("lon", "sec", None),
        P("lon", "sec"),
        P("lon", None),
        P("lon", "sec", None, None),
        P("lon", "sec", None),
    )
    return jax.shard_map(
        per_device,
        mesh=mesh,
        in_specs=placed,
        out_specs=(
            P(None, "sec", "lon"),
            P(None, "sec", "lon"),
            P("lon", "sec", None),
            P("lon", "sec", None),
        ),
        check_vma=False,
    )
```

time: 424 us -> 102 us (0.24)
  waiting for transfers between devices: 281 us -> 0 us
  Pallas kernels: 0 us -> 95.8 us
  local copies, waits for them, and re-layouts: 54.8 us -> 5.62 us
  starting transfers between devices: 35.9 us -> 0 us
  other arithmetic: 32.7 us -> 0 us
  between operations: 15.8 us -> 0.66 us
    unnamed x2 -> x0, waiting for transfers between devices: 183 us -> none
    all_to_all x2 -> x0, waiting for transfers between devices: 98.2 us -> none  [the longest x1 98.2 us: per_device(): lax.all_to_all(record_new[rows_left], 'sec', split_axis=0, concat_axis=0,...]
    pallas_call x0 -> x1, Pallas kernels: none -> 95.8 us  [per_device(): pl.pallas_call(kernel, out_shape=(jax.ShapeDtypeStruct(moisture.shape, F3...]
    gather x3 -> x0, local copies, waits for them, and re-layouts: 51.8 us -> none  [the longest x1 23 us: per_device(): slot_ids = jnp.where(usable, jnp.take(local_slot, rows_left), -1)]
    all_to_all x2 -> x0, starting transfers between devices: 23.2 us -> none  [the longest x1 15.6 us: per_device(): lax.all_to_all(slot_ids, 'sec', split_axis=0, concat_axis=0, tiled=True)]
    scatter-add x1 -> x0, other arithmetic: 22 us -> none  [per_device(): jax.ops.segment_sum(runoff.reshape(-1), cell_reach.reshape(-1), num_segme...]
    ppermute x4 -> x0, starting transfers between devices: 12.7 us -> none  [the longest x2 8.42 us: extended(): lax.ppermute(tail, axis, [(i, (i + 1) % count) for i in range(ends)])]
    convert_element_type x5 -> x0, other arithmetic: 4.72 us -> none  [the longest x1 1.74 us: per_device(): (shifted + reach_runoff[:, None] * unit_hydro[0].astype(jnp.float32)).ast...]
  transfers between devices with their start and end apart: 7 -> 0, of which waited for: 2 -> 0; matrix products, arithmetic and copies ran while one was open for 14% -> 0% of each run, Pallas kernels for 0% -> 0%
where the time goes in v2:
time: 102 us
  Pallas kernels  95.8 us (94%)
  local copies, waits for them, and re-layouts  5.62 us (6%)
    pallas_call x1, Pallas kernels, per_device(): pl.pallas_call(kernel, out_shape=(jax.ShapeDtypeStruct(moisture.shape, F3...  95.8 us
    unnamed x8, local copies, waits for them, and re-layouts  5.62 us

profile of v2, /device:TPU:1, one launch (start us, length us, event | category | flops | bytes accessed | tf_op | source)
XLA Modules:
  0.0 102.1 jit_solution(15766920591670847377)
XLA Ops:
  0.6 95.8 %shard_map.156 = (f32[16,16,256]{2,1,0:T(8,128)}, f32[16,16,256]{2,1,0:T(8,128)}, bf16[2048,256]{1,0:T(8,128)(2,1)}, f32[512,256]{1,0:T(8,128)}) custom-call(f32[16,16,256]{2,1,0:T(8,128)} %moist.1, f32[16,16,256]{2,1,0:T(8,128)} %heat.1, f32[16,16,256]{2,1,0:T(8,128)} %moist_cond.1, f32[16,16,256]{2,1,0:T(8,128)} %heat_cond.1, f32[16,256]{1,0:T(8,128)} %rain.1, ...), custom_call_target="tpu_custom_call" | custom-call | tf_op jit(solution)/shard_map/pallas_call | solution.py:470
  96.4 0.0 copy-start
  96.4 1.8 %copy.21 = f32[16,16,256]{2,1,0:T(8,128)} copy(f32[16,16,256]{2,1,0:T(8,128)} %get-tuple-element.16) | data formatting | bytes 524288
  98.2 1.7 %copy.22 = f32[16,16,256]{2,1,0:T(8,128)} copy(f32[16,16,256]{2,1,0:T(8,128)} %get-tuple-element.17) | data formatting | bytes 524288
  99.9 0.0 copy-done
  99.9 0.0 copy-start.1
  99.9 1.0 copy.23
  100.9 0.4 copy-done.1
  101.3 0.8 copy.24
Async XLA Ops:
  96.4 3.4 %copy-start = (bf16[2048,256]{1,0:T(8,128)(2,1)S(1)}, bf16[2048,256]{1,0:T(8,128)(2,1)}, u32[]{:S(2)}) copy-start(bf16[2048,256]{1,0:T(8,128)(2,1)} %get-tuple-element.10) | copy-start | bytes 3145732
  99.9 1.4 %copy-start.1 = (f32[512,256]{1,0:T(8,128)S(1)}, f32[512,256]{1,0:T(8,128)}, u32[]{:S(2)}) copy-start(f32[512,256]{1,0:T(8,128)} %get-tuple-element.11) | copy-start | bytes 1572868

commit v3 on v2

--- a/solution.py
+++ b/solution.py
@@ -33,65 +33,60 @@
     return jnp.sum(jnp.where(iota(shape, 1) == lane, block, 0.0), axis=1, keepdims=True)
 
 
-def kernel(
-    moist,
-    heat,
-    moist_cond,
-    heat_cond,
-    rain,
-    flux,
-    cells,
-    records,
-    hydro,
-    basins,
-    homes,
-    send_index,
-    send_count,
-    moist_out,
-    heat_out,
-    record_out,
-    inflow,
-    base,
-    inv,
-    back,
-    ratio,
-    row_out,
-    row_in,
-    col_out,
-    col_in,
-    cells_in,
-    value_out,
-    value_in,
-    hi,
-    lo,
-    value,
-    spread,
-    marks,
-    terms_out,
-    terms_in,
-    places,
-    picks,
-    slots,
-    ids_out,
-    ids_in,
-    shifted,
-    hydro_at,
-    rows_out,
-    rows_in,
-    chosen,
-    sums,
-    sums_in,
-    halo_send,
-    halo_recv,
-    pair_send,
-    pair_recv,
-    terms_send,
-    terms_recv,
-    ids_send,
-    ids_recv,
-    rows_send,
-    rows_recv,
-):
+def kernel(*refs):
+    hbm, outs, rest = refs[:13], refs[13:17], refs[17:]
+    local, rest = rest[:13], rest[13:]
+    moist_out, heat_out, record_out, inflow, rest = *rest[:4], rest[4:]
+    moist, heat, moist_cond, heat_cond, rain, flux, cells = local[:7]
+    records, hydro, basins, homes, send_index, send_count = local[7:]
+    (
+        base,
+        inv,
+        back,
+        ratio,
+        row_out,
+        row_in,
+        col_out,
+        col_in,
+        cells_in,
+        value_out,
+        value_in,
+        hi,
+        lo,
+        value,
+        spread,
+        marks,
+        terms_out,
+        terms_in,
+        places,
+        pick_rows,
+        picks,
+        ids_out,
+        ids_in,
+        ids_near,
+        pick,
+        shifted,
+        hydro_at,
+        rows_out,
+        rows_in,
+        rows_near,
+        chosen,
+        chosen_near,
+        load_sem,
+        save_sem,
+        halo_send,
+        halo_recv,
+        pair_send,
+        pair_recv,
+        terms_send,
+        terms_recv,
+        ids_send,
+        ids_recv,
+        rows_send,
+        rows_recv,
+        near_send,
+        near_recv,
+    ) = rest
     layers, lats, width = moist.shape
     chips = rows_out.shape[0]
     cap = rows_out.shape[1]
@@ -124,6 +119,19 @@
     lax.fori_loop(0, chips - 1, greet, 0)
     for peer in ({"sec": up}, {"sec": down}, {"lon": left}, {"lon": right}):
         pl.semaphore_signal(barrier, inc=1, device_id=peer)
+
+    loads = [
+        pltpu.make_async_copy(src, dst, load_sem.at[i])
+        for i, (src, dst) in enumerate(zip(hbm, local))
+    ]
+    for i in (0, 1, 2, 3, 4, 5, 6, 9, 10, 11, 12, 7, 8):
+        loads[i].start()
+
+    def save(i, src):
+        return pltpu.make_async_copy(src, outs[i], save_sem.at[i])
+
+    for i in range(7):
+        loads[i].wait()
 
     lane_e = iota((lats, 128), 1)
     first = jnp.zeros((lats, 128), F32)
@@ -186,46 +194,62 @@
 
     cell_marks(0, cells)
 
-    eye = ones_where(iota((128, 128), 0) == iota((128, 128), 1))
-    flip = ones_where(iota((128, 128), 0) + iota((128, 128), 1) == 127)
-    basin = basins[...]
-    basin_cols = dot_nt(
-        eye, jnp.concatenate([basin // 128, basin % 128], axis=0).astype(F32).astype(BF)
-    )
-    home = homes[...] % (2 * inflow.shape[0])
-    table = jnp.concatenate([home // 256, home % 256], axis=1).astype(F32).astype(BF)
+    for i in range(9, 13):
+        loads[i].wait()
+    home = (homes[...] % (2 * inflow.shape[0])).astype(F32).T.astype(I32)
+    table = jnp.concatenate([home // 256, home % 256], axis=0).astype(F32).astype(BF)
     groups = reaches // 128
 
     def look(m, _):
-        found = dot(ones_where(column(basin_cols, m).astype(I32) == iota((128, 128), 1)), table)
-        at = column(basin_cols, groups + m).astype(I32) == iota((128, 128), 1)
-        high = jnp.sum(jnp.where(at, found[:, :128], 0.0), axis=1, keepdims=True)
-        low = jnp.sum(jnp.where(at, found[:, 128:], 0.0), axis=1, keepdims=True)
-        lane = iota((128, 128), 1)
-        places[pl.ds(pl.multiple_of(m * 128, 128), 128), :] = jnp.where(
-            lane == 0, high, jnp.where(lane == 1, low, 0.0)
-        ).astype(BF)
+        basin = basins[pl.ds(m, 1), :]
+        found = dot(table, ones_where(basin // 128 == iota((128, 128), 0)))
+        at = basin % 128 == iota((128, 128), 0)
+        high = jnp.sum(jnp.where(at, found[:128], 0.0), axis=0, keepdims=True)
+        low = jnp.sum(jnp.where(at, found[128:], 0.0), axis=0, keepdims=True)
+        places[pl.ds(m, 1), :] = high
+        places[pl.ds(groups + m, 1), :] = low
         return 0
 
     lax.fori_loop(0, groups, look, 0)
 
     even = send_index[pl.ds(0, chips, stride=2), :]
     odd = send_index[pl.ds(1, chips, stride=2), :]
+    flip = ones_where(iota((128, 128), 0) + iota((128, 128), 1) == 127)
 
     def halves(x):
-        return jnp.concatenate([x // 256, x % 256], axis=0).astype(F32).astype(BF)
+        return jnp.concatenate([x // 128, x % 128], axis=0).astype(F32)
 
     pick_even = ones_where(
-        iota((2 * chips, 2 * chips), 0) == 2 * (iota((2 * chips, 2 * chips), 1) % chips)
+        iota((2 * chips, 2 * chips), 1) == 2 * (iota((2 * chips, 2 * chips), 0) % chips)
     )
-    counts = dot(
-        jnp.broadcast_to(send_count[...], (8, 2 * chips)).astype(F32).astype(BF), pick_even
+    counts = dot_nt(
+        pick_even, jnp.broadcast_to(send_count[...], (8, 2 * chips)).astype(F32).astype(BF)
     )
-    picks[...] = jnp.where(
-        iota((cap, 2 * chips), 0).astype(F32) < counts[0:1, :],
-        dot_nt(eye, halves(even)),
-        dot_nt(flip, halves(odd)),
+    pick_rows[pl.ds(0, 2 * chips)] = jnp.where(
+        iota((2 * chips, cap), 1).astype(F32) < counts[:, 0:1],
+        halves(even),
+        dot(halves(odd).astype(BF), flip),
     )
+    pick_rows[pl.ds(2 * chips, cap - 2 * chips)] = jnp.zeros((cap - 2 * chips, cap), F32)
+    picks[...] = pick_rows[...].T
+    place_cols = places[...].T.astype(BF)
+
+    def ids_fill(m, _):
+        group = pick_rows[pl.ds(m, 1), :].astype(I32)
+        at = pick_rows[pl.ds(chips + m, 1), :].astype(I32) == iota((128, cap), 0)
+        digit = iota((2 * groups, cap), 0)
+        found = dot(
+            place_cols,
+            jnp.concatenate(
+                [ones_where(digit == group), ones_where(digit == group + groups)], axis=1
+            ),
+        )
+        high = jnp.sum(jnp.where(at, found[:, :cap], 0.0), axis=0, keepdims=True)
+        low = jnp.sum(jnp.where(at, found[:, cap:], 0.0), axis=0, keepdims=True)
+        ids_out[m] = (high * 256.0 + low).astype(I32)
+        return 0
+
+    lax.fori_loop(0, chips, ids_fill, 0)
 
     pl.semaphore_wait(barrier, chips - 1 + 4)
 
@@ -238,7 +262,22 @@
     reach_pair = copy(cells, cells_in, pair_send.at[0], pair_recv.at[0], sec=partner)
     for one in halo:
         one.start()
+    def ids_copy(k):
+        return copy(
+            ids_out.at[target(k)],
+            ids_in.at[k],
+            ids_send.at[k],
+            ids_recv.at[k],
+            sec=target(k) * 2 + core,
+        )
+
+    def ids_start(k, _):
+        ids_copy(k).start()
+        return 0
+
     reach_pair.start()
+    lax.fori_loop(0, chips - 1, ids_start, 0)
+    ids_in[chips - 1] = ids_out[chip]
     reach_pair.wait()
     cell_marks(lats, cells_in)
     for one in halo:
@@ -269,12 +308,12 @@
             prev = source * inv[f, layer] + back[f, layer] * prev
             held.append(prev)
         x = held[-1]
-        out[layers - 1] = x
+        out[pl.ds((layers - 1) * lats, lats), :] = x
         if f == 0:
             runoff = 0.5 * moist_cond[layers - 1] * x
         for layer in range(layers - 2, -1, -1):
             x = held[layer] - ratio[f, layer] * x
-            out[layer] = x
+            out[pl.ds(layer * lats, lats), :] = x
         surface.append(x)
     wet = surface[0] - 1.0
     softplus = jnp.maximum(wet, 0.0) + jnp.log1p(jnp.exp(-jnp.abs(wet)))
@@ -313,43 +352,37 @@
         return 0
 
     lax.fori_loop(0, chips - 1, terms_start, 0)
+    save(0, moist_out).start()
+    save(1, heat_out).start()
     terms_in[chips - 1] = terms_out[chip]
 
+    loads[7].wait()
+    loads[8].wait()
     lane_s = iota((cap, steps), 1)
-
-    def pack(m, ids):
-        at = column(picks[...], m) * 256.0 + column(picks[...], chips + m)
-        pick = ones_where(at.astype(I32) == iota((cap, reaches), 1))
-        place = dot(pick, places[...])
-        hydro_at[m] = dot(pick, hydro[...])
-        moved = pltpu.roll(dot(pick, records[...]), steps - 1, 1)
-        shifted[m] = jnp.where(lane_s == steps - 1, 0.0, moved)
-        place = column(place, 0) * 256.0 + column(place, 1)
-        return jnp.where(iota((cap, 128), 1) == m, place, ids)
-
-    ids = lax.fori_loop(0, chips, pack, jnp.zeros((cap, 128), F32))
-    slots[...] = ids.T.astype(I32)
-
-    def ids_copy(k):
-        return copy(
-            ids_out.at[target(k)],
-            ids_in.at[k],
-            ids_send.at[k],
-            ids_recv.at[k],
-            sec=target(k) * 2 + core,
-        )
-
-    def ids_fill(m, _):
-        ids_out[m] = jnp.broadcast_to(slots[pl.ds(m, 1), :], (8, 128))
-        return 0
-
-    def ids_start(k, _):
-        ids_copy(k).start()
-        return 0
-
-    lax.fori_loop(0, chips, ids_fill, 0)
-    lax.fori_loop(0, chips - 1, ids_start, 0)
-    ids_in[chips - 1] = ids_out[chip]
+    batch = pick.shape[0] // cap
+
+    def pack(i, _):
+        for b in range(batch):
+            at = column(picks[...], i * batch + b) * 128.0
+            at = at + column(picks[...], chips + i * batch + b)
+            pick[pl.ds(b * cap, cap), :] = ones_where(at.astype(I32) == iota((cap, reaches), 1))
+        now = pl.ds(i * batch, batch)
+        hydro_at[now] = dot(pick[...], hydro[...]).reshape(batch, cap, steps)
+        moved = dot(pick[...], records[...])
+        for b in range(batch):
+            one = pltpu.roll(moved[b * cap : (b + 1) * cap], steps - 1, 1)
+            shifted[i * batch + b] = jnp.where(lane_s == steps - 1, 0.0, one)
+        return 0
+
+    lax.fori_loop(0, chips // batch, pack, 0)
+
+    def ids_wait(k, _):
+        ids_copy(k).wait()
+        return 0
+
+    lax.fori_loop(0, chips - 1, ids_wait, 0)
+    ids_pair = copy(ids_in, ids_near, pair_send.at[2], pair_recv.at[2], sec=partner)
+    ids_pair.start()
 
     def terms_wait(k, _):
         terms_copy(k).wait()
@@ -365,9 +398,10 @@
     parts = both.shape[0]
 
     def make_rows(m):
-        octet = column(picks[...], m).astype(I32)
+        index = column(picks[...], m) * 128.0 + column(picks[...], chips + m)
+        octet = index.astype(I32) // 256
         found = dot(ones_where(octet == iota((cap, parts), 1) % (parts // 2)), both)
-        at = column(picks[...], chips + m).astype(I32) == iota((cap, 256), 1)
+        at = index.astype(I32) % 256 == iota((cap, 256), 1)
         scale = jnp.sum(jnp.where(at, found, 0.0), axis=1, keepdims=True)
         return (shifted[m] + scale * hydro_at[m]).astype(BF)
 
@@ -399,47 +433,66 @@
         moved = jnp.where(lane_w == steps - 1, 0.0, moved)
         record_out[rows, :] = (moved + scale * hydro[rows, :].astype(F32)).astype(BF)
 
-    def ids_wait(k, _):
-        ids_copy(k).wait()
-        return 0
-
-    lax.fori_loop(0, chips - 1, ids_wait, 0)
+    save(2, record_out).start()
+    ids_pair.wait()
+    mine = inflow.shape[0]
+    basin_at = iota((mine, 2 * cap), 0) + core * mine
 
     def choose(i, _):
-        got = jnp.concatenate([ids_in[2 * i][0:1, :], ids_in[2 * i + 1][0:1, :]], axis=1)
-        chosen[i] = ones_where(got == iota((sums.shape[0], 2 * cap), 0))
+        for marked, ids in ((chosen, ids_in), (chosen_near, ids_near)):
+            got = jnp.concatenate([ids[2 * i], ids[2 * i + 1]], axis=1)
+            marked[i] = ones_where(got == basin_at)
         return 0
 
     lax.fori_loop(0, chips // 2, choose, 0)
 
-    def gain(i):
-        pair = rows_in[pl.ds(2 * i, 2)].reshape(2 * cap, steps)
-        return dot(chosen[i], pair)
-
+    def gain(i, marked, rows):
+        return dot(marked[i], rows[pl.ds(2 * i, 2)].reshape(2 * cap, steps))
+
+    def near_copy(i):
+        pair = pl.ds(2 * i, 2)
+        return copy(
+            rows_in.at[pair], rows_near.at[pair], near_send.at[i], near_recv.at[i], sec=partner
+        )
+
+    last = chips // 2 - 1
     rows_copy(0).wait()
     rows_copy(1).wait()
-    sums[...] = gain(0)
+    near_copy(0).start()
+    inflow[...] = gain(0, chosen, rows_in)
 
     def add(i, _):
         rows_copy(2 * i).wait()
         rows_copy(2 * i + 1).wait()
-        sums[...] += gain(i)
-        return 0
-
-    lax.fori_loop(1, chips // 2 - 1, add, 0)
+        near_copy(i).start()
+        near_copy(i - 1).wait()
+        inflow[...] += gain(i, chosen, rows_in) + gain(i - 1, chosen_near, rows_near)
+        return 0
+
+    lax.fori_loop(1, last, add, 0)
     rows_copy(chips - 2).wait()
-    sums[...] += gain(chips // 2 - 1)
-    mine = inflow.shape[0]
-    swap = copy(
-        sums.at[pl.ds(pl.multiple_of((1 - core) * mine, mine), mine)],
-        sums_in,
-        pair_send.at[2],
-        pair_recv.at[2],
-        sec=partner,
-    )
-    swap.start()
-    swap.wait()
-    inflow[...] = sums[pl.ds(pl.multiple_of(core * mine, mine), mine), :] + sums_in[...]
+    near_copy(last).start()
+    near_copy(last - 1).wait()
+    inflow[...] += gain(last, chosen, rows_in) + gain(last - 1, chosen_near, rows_near)
+    near_copy(last).wait()
+    inflow[...] += gain(last, chosen_near, rows_near)
+    save(3, inflow).start()
+    for i, done in enumerate((moist_out, heat_out, record_out, inflow)):
+        save(i, done).wait()
+
+
+def hand_over(*refs):
+    srcs, dsts, held, load_sem, save_sem = refs[:4], refs[4:8], refs[8:12], refs[12], refs[13]
+    order = (2, 3, 0, 1)
+    loads = [pltpu.make_async_copy(srcs[i], held[i], load_sem.at[i]) for i in range(4)]
+    saves = [pltpu.make_async_copy(held[i], dsts[i], save_sem.at[i]) for i in range(4)]
+    for i in order:
+        loads[i].start()
+    for i in order:
+        loads[i].wait()
+        saves[i].start()
+    for i in order:
+        saves[i].wait()
 
 
 def per_device(
@@ -467,17 +520,35 @@
     octets = reaches // 256
     vmem = pltpu.VMEM
     sem = pltpu.SemaphoreType.DMA
+    args = (
+        moisture,
+        heat,
+        moist_cond,
+        heat_cond,
+        rain,
+        surface_flux,
+        cell_reach,
+        records[0],
+        unit_hydro[0],
+        down_basin.reshape(reaches // 128, 128),
+        basin_home.reshape(-1, 128),
+        send_index[0, 0],
+        send_count[0],
+    )
+    results = (
+        jax.ShapeDtypeStruct((layers * lats, width), F32),
+        jax.ShapeDtypeStruct((layers * lats, width), F32),
+        jax.ShapeDtypeStruct((reaches, steps), BF),
+        jax.ShapeDtypeStruct((mine, steps), F32),
+    )
+    anywhere = pl.BlockSpec(memory_space=pl.ANY)
     out = pl.pallas_call(
         kernel,
-        out_shape=(
-            jax.ShapeDtypeStruct(moisture.shape, F32),
-            jax.ShapeDtypeStruct(heat.shape, F32),
-            jax.ShapeDtypeStruct((reaches, steps), BF),
-            jax.ShapeDtypeStruct((mine, steps), F32),
-        ),
-        in_specs=[pl.BlockSpec(memory_space=vmem)] * 13,
-        out_specs=tuple([pl.BlockSpec(memory_space=vmem)] * 4),
-        scratch_shapes=[
+        out_shape=results,
+        in_specs=[anywhere] * 13,
+        out_specs=(anywhere,) * 4,
+        scratch_shapes=[vmem(a.shape, a.dtype) for a in args + results]
+        + [
             vmem(field, F32),
             vmem(field, F32),
             vmem(field, F32),
@@ -496,18 +567,22 @@
             vmem((256, 2 * lats * width), BF),
             vmem((chips, octets, 256), BF),
             vmem((chips, octets, 256), BF),
-            vmem((reaches, 128), BF),
-            vmem((cap, 2 * chips), F32),
-            vmem((128, cap), I32),
-            vmem((chips, 8, 128), I32),
-            vmem((chips, 8, 128), I32),
+            vmem((2 * reaches // 128, 128), F32),
+            vmem((cap, cap), F32),
+            vmem((cap, cap), F32),
+            vmem((chips, 1, cap), I32),
+            vmem((chips, 1, cap), I32),
+            vmem((chips, 1, cap), I32),
+            vmem((4 * cap, reaches), BF),
             vmem((chips, cap, steps), F32),
             vmem((chips, cap, steps), F32),
             vmem((chips, cap, steps), BF),
             vmem((chips, cap, steps), BF),
-            vmem((chips // 2, 2 * mine, 2 * cap), BF),
-            vmem((2 * mine, steps), F32),
-            vmem((mine, steps), F32),
+            vmem((chips, cap, steps), BF),
+            vmem((chips // 2, mine, 2 * cap), BF),
+            vmem((chips // 2, mine, 2 * cap), BF),
+            sem((13,)),
+            sem((4,)),
             sem((4,)),
             sem((4,)),
             sem((3,)),
@@ -518,26 +593,22 @@
             sem((chips,)),
             sem((chips,)),
             sem((chips,)),
+            sem((chips // 2,)),
+            sem((chips // 2,)),
         ],
         compiler_params=pltpu.CompilerParams(
             collective_id=0, has_side_effects=True, vmem_limit_bytes=60 * 1024 * 1024
         ),
-    )(
-        moisture,
-        heat,
-        moist_cond,
-        heat_cond,
-        rain,
-        surface_flux,
-        cell_reach,
-        records[0],
-        unit_hydro[0],
-        down_basin.reshape(reaches // 128, 128),
-        basin_home.reshape(-1, 128),
-        send_index[0, 0],
-        send_count[0],
-    )
-    return out[0], out[1], out[2][None], out[3][None]
+    )(*args)
+    out = pl.pallas_call(
+        hand_over,
+        out_shape=results,
+        in_specs=[anywhere] * 4,
+        out_specs=(anywhere,) * 4,
+        scratch_shapes=[vmem(a.shape, a.dtype) for a in results] + [sem((4,)), sem((4,))],
+    )(*out)
+    fields = (layers, lats, width)
+    return out[0].reshape(fields), out[1].reshape(fields), out[2][None], out[3][None]
 
 
 def solution(mesh):

time: 102 us -> 89.9 us (0.88)
  Pallas kernels: 95.8 us -> 89.1 us
  local copies, waits for them, and re-layouts: 5.62 us -> 0 us
    pallas_call x1 -> x2, Pallas kernels: 95.8 us -> 89.1 us  [the longest x1 86.5 us: per_device(): pl.pallas_call(kernel, out_shape=results, in_specs=[anywhere] * 13, out_s...]
    unnamed x8 -> x0, local copies, waits for them, and re-layouts: 5.62 us -> none
where the time goes in v3:
time: 89.9 us; the launch traced here: 89.7 us
  Pallas kernels  89.1 us (99%)
    pallas_call x1, Pallas kernels, per_device(): pl.pallas_call(kernel, out_shape=results, in_specs=[anywhere] * 13, out_s...  86.5 us
    pallas_call x1, Pallas kernels, per_device(): pl.pallas_call(hand_over, out_shape=results, in_specs=[anywhere] * 4, out...  2.6 us

profile of v3, /device:TPU:1, one launch (start us, length us, event | category | flops | bytes accessed | tf_op | source)
XLA Modules:
  0.0 89.7 jit_solution(1071078780228015818)
XLA Ops:
  0.6 86.5 %shard_map.156 = (f32[256,256]{1,0:T(8,128)}, f32[256,256]{1,0:T(8,128)}, bf16[2048,256]{1,0:T(8,128)(2,1)}, f32[512,256]{1,0:T(8,128)}) custom-call(f32[16,16,256]{2,1,0:T(8,128)} %refs_0_.1, f32[16,16,256]{2,1,0:T(8,128)} %refs_1_.1, f32[16,16,256]{2,1,0:T(8,128)} %refs_2_.1, f32[16,16,256]{2,1,0:T(8,128)} %refs_3_.1, f32[16,256]{1,0:T(8,128)} %refs_4_.1, ...), custom_call_target="tpu_custom_call" | custom-call | tf_op jit(solution)/shard_map/pallas_call | solution.py:545
  87.1 2.6 %shard_map.157 = (f32[256,256]{1,0:T(8,128)}, f32[256,256]{1,0:T(8,128)}, bf16[2048,256]{1,0:T(8,128)(2,1)}, f32[512,256]{1,0:T(8,128)}) custom-call(f32[256,256]{1,0:T(8,128)} %get-tuple-element.12.refs_0_, f32[256,256]{1,0:T(8,128)} %get-tuple-element.13.refs_1_, bf16[2048,256]{1,0:T(8,128)(2,1)} %get-tuple-element.14.refs_2_, ...), custom_call_target="tpu_custom_call" | custom-call | tf_op jit(solution)/shard_map/pallas_call | solution.py:603

commit v4 on v3

--- a/solution.py
+++ b/solution.py
@@ -192,65 +192,6 @@
 
         lax.fori_loop(at, at + lats, mark, 0)
 
-    cell_marks(0, cells)
-
-    for i in range(9, 13):
-        loads[i].wait()
-    home = (homes[...] % (2 * inflow.shape[0])).astype(F32).T.astype(I32)
-    table = jnp.concatenate([home // 256, home % 256], axis=0).astype(F32).astype(BF)
-    groups = reaches // 128
-
-    def look(m, _):
-        basin = basins[pl.ds(m, 1), :]
-        found = dot(table, ones_where(basin // 128 == iota((128, 128), 0)))
-        at = basin % 128 == iota((128, 128), 0)
-        high = jnp.sum(jnp.where(at, found[:128], 0.0), axis=0, keepdims=True)
-        low = jnp.sum(jnp.where(at, found[128:], 0.0), axis=0, keepdims=True)
-        places[pl.ds(m, 1), :] = high
-        places[pl.ds(groups + m, 1), :] = low
-        return 0
-
-    lax.fori_loop(0, groups, look, 0)
-
-    even = send_index[pl.ds(0, chips, stride=2), :]
-    odd = send_index[pl.ds(1, chips, stride=2), :]
-    flip = ones_where(iota((128, 128), 0) + iota((128, 128), 1) == 127)
-
-    def halves(x):
-        return jnp.concatenate([x // 128, x % 128], axis=0).astype(F32)
-
-    pick_even = ones_where(
-        iota((2 * chips, 2 * chips), 1) == 2 * (iota((2 * chips, 2 * chips), 0) % chips)
-    )
-    counts = dot_nt(
-        pick_even, jnp.broadcast_to(send_count[...], (8, 2 * chips)).astype(F32).astype(BF)
-    )
-    pick_rows[pl.ds(0, 2 * chips)] = jnp.where(
-        iota((2 * chips, cap), 1).astype(F32) < counts[:, 0:1],
-        halves(even),
-        dot(halves(odd).astype(BF), flip),
-    )
-    pick_rows[pl.ds(2 * chips, cap - 2 * chips)] = jnp.zeros((cap - 2 * chips, cap), F32)
-    picks[...] = pick_rows[...].T
-    place_cols = places[...].T.astype(BF)
-
-    def ids_fill(m, _):
-        group = pick_rows[pl.ds(m, 1), :].astype(I32)
-        at = pick_rows[pl.ds(chips + m, 1), :].astype(I32) == iota((128, cap), 0)
-        digit = iota((2 * groups, cap), 0)
-        found = dot(
-            place_cols,
-            jnp.concatenate(
-                [ones_where(digit == group), ones_where(digit == group + groups)], axis=1
-            ),
-        )
-        high = jnp.sum(jnp.where(at, found[:, :cap], 0.0), axis=0, keepdims=True)
-        low = jnp.sum(jnp.where(at, found[:, cap:], 0.0), axis=0, keepdims=True)
-        ids_out[m] = (high * 256.0 + low).astype(I32)
-        return 0
-
-    lax.fori_loop(0, chips, ids_fill, 0)
-
     pl.semaphore_wait(barrier, chips - 1 + 4)
 
     halo = [
@@ -262,22 +203,8 @@
     reach_pair = copy(cells, cells_in, pair_send.at[0], pair_recv.at[0], sec=partner)
     for one in halo:
         one.start()
-    def ids_copy(k):
-        return copy(
-            ids_out.at[target(k)],
-            ids_in.at[k],
-            ids_send.at[k],
-            ids_recv.at[k],
-            sec=target(k) * 2 + core,
-        )
-
-    def ids_start(k, _):
-        ids_copy(k).start()
-        return 0
-
     reach_pair.start()
-    lax.fori_loop(0, chips - 1, ids_start, 0)
-    ids_in[chips - 1] = ids_out[chip]
+    cell_marks(0, cells)
     reach_pair.wait()
     cell_marks(lats, cells_in)
     for one in halo:
@@ -356,6 +283,30 @@
     save(1, heat_out).start()
     terms_in[chips - 1] = terms_out[chip]
 
+    for i in (11, 12):
+        loads[i].wait()
+    groups = reaches // 128
+
+    even = send_index[pl.ds(0, chips, stride=2), :]
+    odd = send_index[pl.ds(1, chips, stride=2), :]
+    flip = ones_where(iota((128, 128), 0) + iota((128, 128), 1) == 127)
+
+    def halves(x):
+        return jnp.concatenate([x // 128, x % 128], axis=0).astype(F32)
+
+    pick_even = ones_where(
+        iota((2 * chips, 2 * chips), 1) == 2 * (iota((2 * chips, 2 * chips), 0) % chips)
+    )
+    counts = dot_nt(
+        pick_even, jnp.broadcast_to(send_count[...], (8, 2 * chips)).astype(F32).astype(BF)
+    )
+    pick_rows[pl.ds(0, 2 * chips)] = jnp.where(
+        iota((2 * chips, cap), 1).astype(F32) < counts[:, 0:1],
+        halves(even),
+        dot(halves(odd).astype(BF), flip),
+    )
+    pick_rows[pl.ds(2 * chips, cap - 2 * chips)] = jnp.zeros((cap - 2 * chips, cap), F32)
+    picks[...] = pick_rows[...].T
     loads[7].wait()
     loads[8].wait()
     lane_s = iota((cap, steps), 1)
@@ -363,8 +314,8 @@
 
     def pack(i, _):
         for b in range(batch):
-            at = column(picks[...], i * batch + b) * 128.0
-            at = at + column(picks[...], chips + i * batch + b)
+            m = target(i * batch + b)
+            at = column(picks[...], m) * 128.0 + column(picks[...], chips + m)
             pick[pl.ds(b * cap, cap), :] = ones_where(at.astype(I32) == iota((cap, reaches), 1))
         now = pl.ds(i * batch, batch)
         hydro_at[now] = dot(pick[...], hydro[...]).reshape(batch, cap, steps)
@@ -374,15 +325,7 @@
             shifted[i * batch + b] = jnp.where(lane_s == steps - 1, 0.0, one)
         return 0
 
-    lax.fori_loop(0, chips // batch, pack, 0)
-
-    def ids_wait(k, _):
-        ids_copy(k).wait()
-        return 0
-
-    lax.fori_loop(0, chips - 1, ids_wait, 0)
-    ids_pair = copy(ids_in, ids_near, pair_send.at[2], pair_recv.at[2], sec=partner)
-    ids_pair.start()
+    pack(0, 0)
 
     def terms_wait(k, _):
         terms_copy(k).wait()
@@ -397,13 +340,14 @@
     both = jnp.concatenate([coarse.astype(F32), fine.astype(F32)], axis=0).astype(BF)
     parts = both.shape[0]
 
-    def make_rows(m):
+    def make_rows(k):
+        m = target(k)
         index = column(picks[...], m) * 128.0 + column(picks[...], chips + m)
         octet = index.astype(I32) // 256
         found = dot(ones_where(octet == iota((cap, parts), 1) % (parts // 2)), both)
         at = index.astype(I32) % 256 == iota((cap, 256), 1)
         scale = jnp.sum(jnp.where(at, found, 0.0), axis=1, keepdims=True)
-        return (shifted[m] + scale * hydro_at[m]).astype(BF)
+        return (shifted[k] + scale * hydro_at[k]).astype(BF)
 
     def rows_copy(k):
         return copy(
@@ -415,12 +359,70 @@
         )
 
     def rows_start(k, _):
-        rows_out[k] = make_rows(target(k))
+        rows_out[k] = make_rows(k)
         rows_copy(k).start()
         return 0
 
-    lax.fori_loop(0, chips - 1, rows_start, 0)
-    rows_in[chips - 1] = make_rows(chip)
+    lax.fori_loop(0, batch, rows_start, 0)
+
+    for i in (9, 10):
+        loads[i].wait()
+    home = (homes[...] % (2 * inflow.shape[0])).astype(F32).T.astype(I32)
+    table = jnp.concatenate([home // 256, home % 256], axis=0).astype(F32).astype(BF)
+    def look(m, _):
+        basin = basins[pl.ds(m, 1), :]
+        found = dot(table, ones_where(basin // 128 == iota((128, 128), 0)))
+        at = basin % 128 == iota((128, 128), 0)
+        high = jnp.sum(jnp.where(at, found[:128], 0.0), axis=0, keepdims=True)
+        low = jnp.sum(jnp.where(at, found[128:], 0.0), axis=0, keepdims=True)
+        places[pl.ds(m, 1), :] = high
+        places[pl.ds(groups + m, 1), :] = low
+        return 0
+
+    lax.fori_loop(0, groups, look, 0)
+
+    place_cols = places[...].T.astype(BF)
+
+    def ids_fill(m, _):
+        group = pick_rows[pl.ds(m, 1), :].astype(I32)
+        at = pick_rows[pl.ds(chips + m, 1), :].astype(I32) == iota((128, cap), 0)
+        digit = iota((2 * groups, cap), 0)
+        found = dot(
+            place_cols,
+            jnp.concatenate(
+                [ones_where(digit == group), ones_where(digit == group + groups)], axis=1
+            ),
+        )
+        high = jnp.sum(jnp.where(at, found[:, :cap], 0.0), axis=0, keepdims=True)
+        low = jnp.sum(jnp.where(at, found[:, cap:], 0.0), axis=0, keepdims=True)
+        ids_out[m] = (high * 256.0 + low).astype(I32)
+        return 0
+
+    lax.fori_loop(0, chips, ids_fill, 0)
+
+    def ids_copy(k):
+        return copy(
+            ids_out.at[target(k)],
+            ids_in.at[k],
+            ids_send.at[k],
+            ids_recv.at[k],
+            sec=target(k) * 2 + core,
+        )
+
+    def ids_start(k, _):
+        ids_copy(k).start()
+        return 0
+
+    lax.fori_loop(0, chips - 1, ids_start, 0)
+    ids_in[chips - 1] = ids_out[chip]
+
+    def more(i, _):
+        pack(i, 0)
+        lax.fori_loop(i * batch, jnp.minimum((i + 1) * batch, chips - 1), rows_start, 0)
+        return 0
+
+    lax.fori_loop(1, chips // batch, more, 0)
+    rows_in[chips - 1] = make_rows(chips - 1)
 
     diagonal = iota((256, 256), 0) == iota((256, 256), 1)
     lane_w = iota((256, steps), 1)
@@ -434,6 +436,14 @@
         record_out[rows, :] = (moved + scale * hydro[rows, :].astype(F32)).astype(BF)
 
     save(2, record_out).start()
+    def ids_wait(k, _):
+        ids_copy(k).wait()
+        return 0
+
+    lax.fori_loop(0, chips - 1, ids_wait, 0)
+    ids_pair = copy(ids_in, ids_near, pair_send.at[2], pair_recv.at[2], sec=partner)
+    ids_pair.start()
+
     ids_pair.wait()
     mine = inflow.shape[0]
     basin_at = iota((mine, 2 * cap), 0) + core * mine

time: 89.9 us -> 88.1 us (0.980)
  Pallas kernels: 89.1 us -> 87.3 us
    pallas_call x1, Pallas kernels: 86.5 us -> 84.7 us  [per_device(): pl.pallas_call(kernel, out_shape=results, in_specs=[anywhere] * 13, out_s...]
where the time goes in v4:
time: 88.1 us; the launch traced here: 87.9 us
  Pallas kernels  87.3 us (99%)
    pallas_call x1, Pallas kernels, per_device(): pl.pallas_call(kernel, out_shape=results, in_specs=[anywhere] * 13, out_s...  84.7 us
    pallas_call x1, Pallas kernels, per_device(): pl.pallas_call(hand_over, out_shape=results, in_specs=[anywhere] * 4, out...  2.6 us

profile of v4, /device:TPU:1, one launch (start us, length us, event | category | flops | bytes accessed | tf_op | source)
XLA Modules:
  0.0 87.9 jit_solution(11552968697754088766)
XLA Ops:
  0.6 84.7 %shard_map.156 = (f32[256,256]{1,0:T(8,128)}, f32[256,256]{1,0:T(8,128)}, bf16[2048,256]{1,0:T(8,128)(2,1)}, f32[512,256]{1,0:T(8,128)}) custom-call(f32[16,16,256]{2,1,0:T(8,128)} %refs_0_.1, f32[16,16,256]{2,1,0:T(8,128)} %refs_1_.1, f32[16,16,256]{2,1,0:T(8,128)} %refs_2_.1, f32[16,16,256]{2,1,0:T(8,128)} %refs_3_.1, f32[16,256]{1,0:T(8,128)} %refs_4_.1, ...), custom_call_target="tpu_custom_call" | custom-call | tf_op jit(solution)/shard_map/pallas_call | solution.py:555
  85.3 2.6 %shard_map.157 = (f32[256,256]{1,0:T(8,128)}, f32[256,256]{1,0:T(8,128)}, bf16[2048,256]{1,0:T(8,128)(2,1)}, f32[512,256]{1,0:T(8,128)}) custom-call(f32[256,256]{1,0:T(8,128)} %get-tuple-element.12.refs_0_, f32[256,256]{1,0:T(8,128)} %get-tuple-element.13.refs_1_, bf16[2048,256]{1,0:T(8,128)(2,1)} %get-tuple-element.14.refs_2_, ...), custom_call_target="tpu_custom_call" | custom-call | tf_op jit(solution)/shard_map/pallas_call | solution.py:613

commit v5 on v4

--- a/solution.py
+++ b/solution.py
@@ -130,7 +130,7 @@
     def save(i, src):
         return pltpu.make_async_copy(src, outs[i], save_sem.at[i])
 
-    for i in range(7):
+    for i in range(2):
         loads[i].wait()
 
     lane_e = iota((lats, 128), 1)
@@ -147,6 +147,8 @@
     col_out[0] = first
     col_out[1] = last
 
+    for i in range(2, 7):
+        loads[i].wait()
     row_at, lane_at = iota((lats, width), 0), iota((lats, width), 1)
     for f, (field, cond, extra) in enumerate(
         ((moist, moist_cond, rain), (heat, heat_cond, flux))
@@ -466,6 +468,15 @@
         )
 
     last = chips // 2 - 1
+
+    def near_one(k, n):
+        return copy(
+            rows_in.at[k], rows_near.at[k], near_send.at[n], near_recv.at[n], sec=partner
+        )
+
+    own_near = near_one(chips - 1, last + 1)
+    last_near = near_one(chips - 2, last)
+    own_near.start()
     rows_copy(0).wait()
     rows_copy(1).wait()
     near_copy(0).start()
@@ -481,10 +492,11 @@
 
     lax.fori_loop(1, last, add, 0)
     rows_copy(chips - 2).wait()
-    near_copy(last).start()
+    last_near.start()
     near_copy(last - 1).wait()
     inflow[...] += gain(last, chosen, rows_in) + gain(last - 1, chosen_near, rows_near)
-    near_copy(last).wait()
+    own_near.wait()
+    last_near.wait()
     inflow[...] += gain(last, chosen_near, rows_near)
     save(3, inflow).start()
     for i, done in enumerate((moist_out, heat_out, record_out, inflow)):
@@ -493,16 +505,24 @@
 
 def hand_over(*refs):
     srcs, dsts, held, load_sem, save_sem = refs[:4], refs[4:8], refs[8:12], refs[12], refs[13]
-    order = (2, 3, 0, 1)
-    loads = [pltpu.make_async_copy(srcs[i], held[i], load_sem.at[i]) for i in range(4)]
-    saves = [pltpu.make_async_copy(held[i], dsts[i], save_sem.at[i]) for i in range(4)]
-    for i in order:
-        loads[i].start()
-    for i in order:
-        loads[i].wait()
-        saves[i].start()
-    for i in order:
-        saves[i].wait()
+    loads, saves = [], []
+    for i, parts in ((2, 4), (3, 2), (0, 1), (1, 1)):
+        rows = held[i].shape[0] // parts
+        for p in range(parts):
+            at, n = pl.ds(p * rows, rows), len(loads)
+            loads.append(
+                pltpu.make_async_copy(srcs[i].at[at], held[i].at[at], load_sem.at[n])
+            )
+            saves.append(
+                pltpu.make_async_copy(held[i].at[at], dsts[i].at[at], save_sem.at[n])
+            )
+    for one in loads:
+        one.start()
+    for load, save in zip(loads, saves):
+        load.wait()
+        save.start()
+    for one in saves:
+        one.wait()
 
 
 def per_device(
@@ -603,8 +623,8 @@
             sem((chips,)),
             sem((chips,)),
             sem((chips,)),
-            sem((chips // 2,)),
-            sem((chips // 2,)),
+            sem((chips // 2 + 1,)),
+            sem((chips // 2 + 1,)),
         ],
         compiler_params=pltpu.CompilerParams(
             collective_id=0, has_side_effects=True, vmem_limit_bytes=60 * 1024 * 1024
@@ -615,7 +635,7 @@
         out_shape=results,
         in_specs=[anywhere] * 4,
         out_specs=(anywhere,) * 4,
-        scratch_shapes=[vmem(a.shape, a.dtype) for a in results] + [sem((4,)), sem((4,))],
+        scratch_shapes=[vmem(a.shape, a.dtype) for a in results] + [sem((8,)), sem((8,))],
     )(*out)
     fields = (layers, lats, width)
     return out[0].reshape(fields), out[1].reshape(fields), out[2][None], out[3][None]

time: 88.1 us -> 87.8 us (level)
  no operation moved by 1% of the time
where the time goes in v5:
time: 87.8 us; the launch traced here: 87.6 us
  Pallas kernels  87 us (99%)
    pallas_call x1, Pallas kernels, per_device(): pl.pallas_call(kernel, out_shape=results, in_specs=[anywhere] * 13, out_s...  84.6 us
    pallas_call x1, Pallas kernels, per_device(): pl.pallas_call(hand_over, out_shape=results, in_specs=[anywhere] * 4, out...  2.4 us

profile of v5, /device:TPU:1, one launch (start us, length us, event | category | flops | bytes accessed | tf_op | source)
XLA Modules:
  0.0 87.6 jit_solution(9036090472790005368)
XLA Ops:
  0.6 84.6 %shard_map.156 = (f32[256,256]{1,0:T(8,128)}, f32[256,256]{1,0:T(8,128)}, bf16[2048,256]{1,0:T(8,128)(2,1)}, f32[512,256]{1,0:T(8,128)}) custom-call(f32[16,16,256]{2,1,0:T(8,128)} %refs_0_.1, f32[16,16,256]{2,1,0:T(8,128)} %refs_1_.1, f32[16,16,256]{2,1,0:T(8,128)} %refs_2_.1, f32[16,16,256]{2,1,0:T(8,128)} %refs_3_.1, f32[16,256]{1,0:T(8,128)} %refs_4_.1, ...), custom_call_target="tpu_custom_call" | custom-call | tf_op jit(solution)/shard_map/pallas_call | solution.py:575
  85.2 2.4 %shard_map.157 = (f32[256,256]{1,0:T(8,128)}, f32[256,256]{1,0:T(8,128)}, bf16[2048,256]{1,0:T(8,128)(2,1)}, f32[512,256]{1,0:T(8,128)}) custom-call(f32[256,256]{1,0:T(8,128)} %get-tuple-element.12.refs_0_, f32[256,256]{1,0:T(8,128)} %get-tuple-element.13.refs_1_, bf16[2048,256]{1,0:T(8,128)(2,1)} %get-tuple-element.14.refs_2_, ...), custom_call_target="tpu_custom_call" | custom-call | tf_op jit(solution)/shard_map/pallas_call | solution.py:633
